TPU v7x, 32 devices: a whole 2x2x4 slice. The times are simulated.
32 devices in a mesh: grp: 2 (over core), tp: 8 (over z, y), dp: 2 (over x).
Axes of the slice: x: 2, y: 2, z: 4, core: 2. Of those that a mesh axis runs over, the one named last changes fastest.
Arguments:
- base_inputs: bfloat16 [3, 128, 8192], P(None, 'dp', ('grp', 'tp')), may hold values from -6 to 6
- small_inputs: bfloat16 [2, 3, 128, 4096], P('grp', None, 'dp', 'tp'), may hold values from -6 to 6
- base_norm_gain: float32 [8192], replicated, may hold values from 0.1 to 1.9
- base_query: bfloat16 [8192, 8192], P(None, ('grp', 'tp')), may hold values from -0.0625 to 0.0625
- base_keys_values: bfloat16 [2, 8192, 1024], P(None, None, ('grp', 'tp')), may hold values from -0.0625 to 0.0625
- base_output: bfloat16 [8192, 8192], P(('grp', 'tp')), may hold values from -0.0625 to 0.0625
- base_cache: bfloat16 [2, 128, 1024, 128], P(None, 'dp', ('grp', 'tp')), may hold values from -600 to 600
- base_final_gain: float32 [8192], replicated, may hold values from 0.1 to 1.9
- base_unembed: bfloat16 [16384, 8192], P(('grp', 'tp')), may hold values from -20 to 20
- small_norm_gain: float32 [2, 4096], P('grp'), may hold values from 0.1 to 1.9
- small_projections: bfloat16 [2, 3, 4096, 4096], P('grp', None, None, 'tp'), may hold values from -0.09375 to 0.09375
- small_output: bfloat16 [2, 4096, 4096], P('grp', 'tp'), may hold values from -0.09375 to 0.09375
- small_cache: bfloat16 [2, 2, 128, 4096, 128], P('grp', None, 'dp', 'tp'), may hold values from -600 to 600
- small_final_gain: float32 [2, 4096], P('grp'), may hold values from 0.1 to 1.9
- small_unembed: bfloat16 [2, 2, 8192, 4096], P('grp', None, 'tp'), may hold values from -0.1875 to 0.1875
- lengths: int32 [128], P('dp'), may hold values from 1 to 128, as said below
- next_tokens: int32 [3, 128], P(None, 'dp'), may hold values from 0 to 16383
Outputs:
- log_probs: float32 [3, 128, 16384], P(None, 'dp', ('grp', 'tp'))
- chosen_total: float32 [128], P('dp')
Inputs may be any that keep to these rules, and one draw needn't show every extreme that they name: `lengths`: some row holds 128 cached positions.
All inputs are finite; a program needn't handle non-finite values.
Results may differ from a plain program's by a relative error of at most 0.0035.
Values may be sent and summed in bfloat16 or wider, within the bound.
A program may use at most 256 MiB of HBM per device.

v0:
```python
import math

import jax
import jax.numpy as jnp
from jax import lax
from jax.sharding import PartitionSpec as P

HD = 128
STEPS = 3
CACHE = 128


EPSILON = 1e-05
NEGATIVE = -1e30


def partner(array, axis, bit):
    return lax.ppermute(array, axis, [(i, i ^ 1 << bit) for i in range(lax.axis_size(axis))])


def rotate_pairs(values, positions, first_pair, head_size):
    pair_count = values.shape[-1] // 2
    pair_index = (first_pair + jnp.arange(pair_count)).astype(jnp.float32)
    frequency = jnp.exp(pair_index * (-2.0 * math.log(10000.0) / head_size))
    angles = positions.astype(jnp.float32)[:, None] * frequency[None, :]
    angles = angles.reshape((values.shape[0],) + (1,) * (values.ndim - 2) + (pair_count,))
    cosine = jnp.cos(angles)
    sine_part = jnp.sin(angles)
    paired = values.reshape(values.shape[:-1] + (pair_count, 2))
    even_part = paired[..., 0]
    odd_part = paired[..., 1]
    turned = jnp.stack(
        [even_part * cosine - odd_part * sine_part, even_part * sine_part + odd_part * cosine],
        axis=-1,
    )
    return turned.reshape(values.shape)


def norm_rows(values, gain_row):
    values = values.astype(jnp.float32)
    scaling = lax.rsqrt(jnp.mean(values * values, axis=-1, keepdims=True) + EPSILON)
    return (values * scaling * gain_row).astype(jnp.bfloat16)


def attention_weights(cached_scores, fresh_scores, visible, head_size):
    factor = 1.0 / math.sqrt(head_size)
    cached_scores = jnp.where(visible, cached_scores * factor, NEGATIVE)
    fresh_scores = fresh_scores * factor
    row_max = jnp.maximum(
        jnp.max(cached_scores, axis=-1, keepdims=True),
        jnp.max(fresh_scores, axis=-1, keepdims=True),
    )
    cached_exp = jnp.exp(cached_scores - row_max)
    fresh_exp = jnp.exp(fresh_scores - row_max)
    totals = jnp.sum(cached_exp, axis=-1, keepdims=True) + jnp.sum(
        fresh_exp, axis=-1, keepdims=True
    )
    return ((cached_exp / totals).astype(jnp.bfloat16), (fresh_exp / totals).astype(jnp.bfloat16))


def sum_slices(scores, share_count):
    for bit_index in range(share_count.bit_length() - 1):
        scores = scores + partner(scores, "tp", bit_index)
    return scores


def body(
    base_inputs,
    small_inputs,
    base_norm_gain,
    base_query,
    base_keys_values,
    base_output,
    base_cache,
    base_final_gain,
    base_unembed,
    small_norm_gain,
    small_projections,
    small_output,
    small_cache,
    small_final_gain,
    small_unembed,
    lengths,
    next_tokens,
):
    row_count = lengths.shape[0]
    slice_width = base_keys_values.shape[2]
    share_count = HD // slice_width
    group_size = base_query.shape[1] // slice_width
    slice_index = lax.axis_index("tp") % share_count
    first_pair = slice_index * (slice_width // 2)
    block_index = lax.axis_index(("grp", "tp"))
    vocab_width = base_unembed.shape[0]
    small_heads = small_projections.shape[3] // HD
    base_full = lax.all_gather(base_inputs, ("grp", "tp"), axis=2, tiled=True)
    small_full = lax.all_gather(small_inputs[0], "tp", axis=2, tiled=True)
    visible = (jnp.arange(CACHE)[None, :] < lengths[:, None])[:, None, :]
    base_keys_cache = base_cache[0]
    base_values_cache = base_cache[1]
    small_keys_cache = small_cache[0, 0].reshape(row_count, small_heads, HD, CACHE)
    small_values_cache = small_cache[0, 1].reshape(row_count, small_heads, HD, CACHE)
    small_table = small_unembed[0].reshape(-1, small_unembed.shape[3])
    base_new_keys = []
    base_new_values = []
    small_new_keys = []
    small_new_values = []
    log_steps = []
    chosen_total = jnp.zeros((row_count,), jnp.float32)
    for step_index in range(STEPS):
        positions = lengths + step_index
        small_normed = norm_rows(small_full[step_index], small_norm_gain[0])
        small_queries = jnp.dot(
            small_normed, small_projections[0, 0], preferred_element_type=jnp.float32
        ).reshape(row_count, small_heads, HD)
        small_queries = rotate_pairs(small_queries, positions, 0, HD).astype(jnp.bfloat16)
        small_key = jnp.dot(
            small_normed, small_projections[0, 1], preferred_element_type=jnp.float32
        ).reshape(row_count, small_heads, HD)
        small_new_keys.append(rotate_pairs(small_key, positions, 0, HD).astype(jnp.bfloat16))
        small_value = jnp.dot(
            small_normed, small_projections[0, 2], preferred_element_type=jnp.float32
        ).reshape(row_count, small_heads, HD)
        small_new_values.append(small_value.astype(jnp.bfloat16))
        small_fresh_keys = jnp.stack(small_new_keys, axis=-1)
        small_fresh_values = jnp.stack(small_new_values, axis=-1)
        small_cached_scores = jnp.einsum(
            "rhd,rhdl->rhl", small_queries, small_keys_cache, preferred_element_type=jnp.float32
        )
        small_fresh_scores = jnp.einsum(
            "rhd,rhdn->rhn", small_queries, small_fresh_keys, preferred_element_type=jnp.float32
        )
        small_cached_weights, small_fresh_weights = attention_weights(
            small_cached_scores, small_fresh_scores, visible, HD
        )
        small_head_values = jnp.einsum(
            "rhl,rhdl->rhd",
            small_cached_weights,
            small_values_cache,
            preferred_element_type=jnp.float32,
        )
        small_head_values = small_head_values + jnp.einsum(
            "rhn,rhdn->rhd",
            small_fresh_weights,
            small_fresh_values,
            preferred_element_type=jnp.float32,
        )
        small_head_values = small_head_values.astype(jnp.bfloat16).reshape(
            row_count, small_heads * HD
        )
        small_partial = jnp.dot(
            small_head_values, small_output[0], preferred_element_type=jnp.float32
        )
        small_mixed = lax.psum(small_partial, "tp")
        small_hidden = small_full[step_index].astype(jnp.float32) + small_mixed
        small_final = norm_rows(small_hidden, small_final_gain[0])
        small_logits = lax.dot_general(
            small_final, small_table, (((1,), (1,)), ((), ())), preferred_element_type=jnp.float32
        )
        small_logits = small_logits.reshape(row_count, 2, small_table.shape[0] // 2)
        paired_logits = lax.all_to_all(
            small_logits[None], "grp", split_axis=2, concat_axis=0, tiled=True
        )
        normed = norm_rows(base_full[step_index], base_norm_gain)
        queries = jnp.dot(normed, base_query, preferred_element_type=jnp.float32).reshape(
            row_count, group_size, slice_width
        )
        queries = rotate_pairs(queries, positions, first_pair, HD).astype(jnp.bfloat16)
        new_key = jnp.dot(normed, base_keys_values[0], preferred_element_type=jnp.float32)
        key_now = rotate_pairs(new_key, positions, first_pair, HD).astype(jnp.bfloat16)
        value_now = jnp.dot(normed, base_keys_values[1], preferred_element_type=jnp.float32).astype(
            jnp.bfloat16
        )
        base_new_keys.append(key_now)
        base_new_values.append(value_now)
        fresh_keys = jnp.stack(base_new_keys, axis=-1)
        fresh_values = jnp.stack(base_new_values, axis=-1)
        cached_scores = jnp.einsum(
            "rgd,rdl->rgl", queries, base_keys_cache, preferred_element_type=jnp.float32
        )
        fresh_scores = jnp.einsum(
            "rgd,rdn->rgn", queries, fresh_keys, preferred_element_type=jnp.float32
        )
        both_scores = sum_slices(
            jnp.concatenate([cached_scores, fresh_scores], axis=-1), share_count
        )
        cached_weights, fresh_weights = attention_weights(
            both_scores[..., :CACHE], both_scores[..., CACHE:], visible, HD
        )
        head_values = jnp.einsum(
            "rgl,rdl->rgd", cached_weights, base_values_cache, preferred_element_type=jnp.float32
        )
        head_values = head_values + jnp.einsum(
            "rgn,rdn->rgd", fresh_weights, fresh_values, preferred_element_type=jnp.float32
        )
        head_values = head_values.astype(jnp.bfloat16).reshape(row_count, group_size * slice_width)
        partial_value = jnp.dot(head_values, base_output, preferred_element_type=jnp.float32)
        mixed_sum = lax.psum(partial_value, ("grp", "tp"))
        hidden = base_full[step_index].astype(jnp.float32) + mixed_sum
        final_rows = norm_rows(hidden, base_final_gain)
        base_logits = lax.dot_general(
            final_rows, base_unembed, (((1,), (1,)), ((), ())), preferred_element_type=jnp.float32
        )
        steered = base_logits + paired_logits[0, :, 0] - paired_logits[1, :, 0]
        local_max = jnp.max(steered, axis=-1)
        token_local = next_tokens[step_index] - block_index * vocab_width
        token_hit = jnp.arange(vocab_width)[None, :] == token_local[:, None]
        picked_local = jnp.sum(jnp.where(token_hit, steered, 0.0), axis=-1)
        row_max = lax.pmax(local_max, ("grp", "tp"))
        exp_total, picked = lax.psum(
            (jnp.sum(jnp.exp(steered - row_max[:, None]), axis=-1), picked_local), ("grp", "tp")
        )
        log_norm = row_max + jnp.log(exp_total)
        log_steps.append(steered - log_norm[:, None])
        chosen_total = chosen_total + picked - log_norm
    return (jnp.stack(log_steps, axis=0), chosen_total)


def solution(mesh):
    placed = (
        P(None, "dp", ("grp", "tp")),
        P("grp", None, "dp", "tp"),
        P(),
        P(None, ("grp", "tp")),
        P(None, None, ("grp", "tp")),
        P(("grp", "tp"), None),
        P(None, "dp", ("grp", "tp"), None),
        P(),
        P(("grp", "tp"), None),
        P("grp", None),
        P("grp", None, None, "tp"),
        P("grp", "tp", None),
        P("grp", None, "dp", "tp", None),
        P("grp", None),
        P("grp", None, "tp", None),
        P("dp"),
        P(None, "dp"),
    )
    return jax.shard_map(
        body,
        mesh=mesh,
        in_specs=placed,
        out_specs=(P(None, "dp", ("grp", "tp")), P("dp")),
        check_vma=False,
    )
```

profile of v0, /device:TPU:0, one launch (start us, length us, event | category | flops | bytes accessed | tf_op | source)
XLA Modules:
  0.0 649.0 jit_solution(7503122877806506709)
XLA Ops:
  8.8 9.1 %slice_bitcast_fusion.1 = (bf16[512,4096]{0,1:T(8,128)(2,1)}, bf16[512,4096]{0,1:T(8,128)(2,1)}, bf16[512,4096]{0,1:T(8,128)(2,1)}) fusion(bf16[1,3,4096,512]{3,2,1,0:T(8,128)(2,1)} %param.27), kind=kLoop, calls=%fused_computation.19 | loop fusion | bytes 25165824 | tf_op jit(solution)/shard_map/dot_general | solution.py:116
  17.8 6.4 copy.294
  24.3 7.6 %dot_general.221 = bf16[4,64,2,4096]{3,2,1,0:T(2,128)(2,1)} reshape(bf16[512,4096]{1,0:T(8,128)(2,1)} %copy.294) | data formatting | bytes 8388608 | tf_op jit(solution)/shard_map/dot_general | solution.py:116
  31.9 6.4 copy.297
  38.4 6.5 copy.291
  44.8 7.6 %dot_general.217 = bf16[4,64,2,4096]{3,2,1,0:T(2,128)(2,1)} reshape(bf16[512,4096]{1,0:T(8,128)(2,1)} %copy.291) | data formatting | bytes 8388608 | tf_op jit(solution)/shard_map/dot_general | solution.py:112
  53.1 11.8 %fusion.262 = (bf16[1,1,64,512,128]{4,3,2,1,0:T(8,128)(2,1)}, bf16[1,1,64,512,128]{4,3,2,1,0:T(8,128)(2,1)}) fusion(bf16[1,2,64,512,128]{4,3,2,1,0:T(8,128)(2,1)} %param.29), kind=kLoop, calls=%fused_computation.419 | loop fusion | bytes 33554432 | tf_op jit(solution)/shard_map/slice | solution.py:100
  66.2 7.3 %fusion.28 = f32[64,4,64,2]{2,0,3,1:T(8,128)S(1)} fusion(bf16[4,64,2,4096]{3,2,1,0:T(2,128)(2,1)} %dot_general.217, f32[4096]{0:T(1024)S(1)} %bitcast.550, f32[64]{0:T(128)S(1)} %add_rsqrt_fusion.9, bf16[1,3,64,4096]{3,2,1,0:T(8,128)(2,1)} %all-gather.6.cloned.1.call-done), kind=kOutput, calls=%fused_computation.31 | convolution fusion | flops 269484032 | bytes 4866304 | tf_op jit(solution)/shard_map/dot_general | solution.py:112
  73.7 7.1 %fusion.22 = f32[64,4,64,2]{2,0,3,1:T(8,128)S(1)} fusion(bf16[4,64,2,4096]{3,2,1,0:T(2,128)(2,1)} %dot_general.221, f32[4096]{0:T(1024)S(1)} %bitcast.551, f32[64]{0:T(128)S(1)} %add_rsqrt_fusion.9, bf16[1,3,64,4096]{3,2,1,0:T(8,128)(2,1)S(1)} %copy-done.5), kind=kOutput, calls=%fused_computation.25 | convolution fusion | flops 269484032 | bytes 4866560 | tf_op jit(solution)/shard_map/dot_general | solution.py:116
  81.3 5.6 fusion.269
  87.4 8.3 %fusion.173 = f32[64,4,1,128]{3,2,1,0:T(1,128)S(1)} fusion(bf16[64,4,128,128]{3,2,1,0:T(8,128)(2,1)} %bitcast.520, bf16[64,4,128,1]{2,0,1,3:T(8,128)(2,1)S(1)} %fusion.197), kind=kOutput, calls=%fused_computation.254 | convolution fusion | flops 8388608 | bytes 8585216 | tf_op jit(solution)/shard_map/rhl,rhdl->rhd/dot_general | solution.py:135
  100.5 11.4 %copy.275 = bf16[512,8192]{1,0:T(8,128)(2,1)} copy(bf16[512,8192]{0,1:T(8,128)(2,1)} %bitcast.528) | data formatting | bytes 16777216 | tf_op jit(solution)/shard_map/dot_general | solution.py:164
  111.9 14.1 %dot_general.201 = bf16[8,32,2,8192]{3,2,1,0:T(2,128)(2,1)} reshape(bf16[512,8192]{1,0:T(8,128)(2,1)} %copy.275) | data formatting | bytes 16777216 | tf_op jit(solution)/shard_map/dot_general | solution.py:164
  130.4 61.5 %all-reduce.8.cloned.1.call-done = f32[64,4096]{1,0:T(8,128)} async-done(((f32[64,4096]{1,0:T(8,128)}), f32[64,4096]{1,0:T(8,128)}) %all-reduce.8.cloned.1.call-update) | async-done | bytes 1048592 | tf_op jit(solution)/shard_map/psum | solution.py:153
  194.1 7.2 %fusion.20 = f32[64,4,64,2]{2,0,3,1:T(8,128)S(1)} fusion(bf16[4,64,2,4096]{3,2,1,0:T(2,128)(2,1)} %dot_general.221, f32[64]{0:T(128)S(1)} %get-tuple-element.123, f32[4096]{0:T(1024)S(1)} %bitcast.553, bf16[1,3,64,4096]{3,2,1,0:T(8,128)(2,1)S(1)} %copy-done.5), kind=kOutput, calls=%fused_computation.23 | convolution fusion | flops 269484032 | bytes 4866560 | tf_op jit(solution)/shard_map/dot_general | solution.py:116
  206.9 5.6 fusion.271
  213.0 7.2 %fusion.18 = f32[64,4,64,2]{2,0,3,1:T(8,128)S(1)} fusion(bf16[4,64,2,4096]{3,2,1,0:T(2,128)(2,1)} %dot_general.221, f32[64]{0:T(128)S(1)} %get-tuple-element.122, f32[4096]{0:T(1024)S(1)} %bitcast.555, bf16[1,3,64,4096]{3,2,1,0:T(8,128)(2,1)S(1)} %copy-done.5), kind=kOutput, calls=%fused_computation.21 | convolution fusion | flops 269484032 | bytes 4866560 | tf_op jit(solution)/shard_map/dot_general | solution.py:116
  239.5 7.9 %fusion.169 = f32[64,4,1,128]{3,2,1,0:T(1,128)S(1)} fusion(bf16[64,4,128,128]{3,2,1,0:T(8,128)(2,1)} %bitcast.521, bf16[64,4,128,1]{2,0,1,3:T(8,128)(2,1)S(1)} %get-tuple-element.83), kind=kOutput, calls=%fused_computation.250 | convolution fusion | flops 8388608 | bytes 8585216 | tf_op jit(solution)/shard_map/rhl,rhdl->rhd/dot_general | solution.py:135
  260.4 9.4 %fusion.8 = f32[64,8,32,2]{0,2,3,1:T(8,128)S(1)} fusion(bf16[8,32,2,8192]{3,2,1,0:T(2,128)(2,1)} %dot_general.201, f32[64]{0:T(128)S(1)} %get-tuple-element.125, f32[8192]{0:T(1024)S(1)} %copy-done.49, bf16[3,64,8192]{2,1,0:T(8,128)(2,1)S(1)} %copy-done.4), kind=kOutput, calls=%fused_computation.8 | convolution fusion | flops 538968064 | bytes 9601536 | tf_op jit(solution)/shard_map/dot_general | solution.py:164
  288.6 9.2 %fusion.10 = f32[64,8,32,2]{0,2,3,1:T(8,128)S(1)} fusion(bf16[8,32,2,8192]{3,2,1,0:T(2,128)(2,1)} %dot_general.201, f32[8192]{0:T(1024)} %param.19, f32[64]{0:T(128)} %copy-done.52, bf16[3,64,8192]{2,1,0:T(8,128)(2,1)S(1)} %copy-done.4), kind=kOutput, calls=%fused_computation.10 | convolution fusion | flops 538968064 | bytes 9601280 | tf_op jit(solution)/shard_map/dot_general | solution.py:164
  306.2 9.0 %fusion.6 = f32[64,8,32,2]{0,2,3,1:T(8,128)S(1)} fusion(bf16[8,32,2,8192]{3,2,1,0:T(2,128)(2,1)} %dot_general.201, f32[64]{0:T(128)} %get-tuple-element.124, f32[8192]{0:T(1024)} %param.19, bf16[3,64,8192]{2,1,0:T(8,128)(2,1)S(1)} %copy-done.4), kind=kOutput, calls=%fused_computation.6 | convolution fusion | flops 538968064 | bytes 9601280 | tf_op jit(solution)/shard_map/dot_general | solution.py:164
  369.8 6.5 fusion.272
  376.3 6.5 %fusion.268 = f32[64,8192]{1,0:T(8,128)} fusion(bf16[64,512]{1,0:T(8,128)(2,1)S(1)} %copy-done.14, bf16[512,8192]{1,0:T(8,128)(2,1)} %param.22), kind=kOutput, calls=%fused_computation.425 | convolution fusion | flops 536870912 | bytes 10551296 | tf_op jit(solution)/shard_map/dot_general | solution.py:196
  386.3 13.1 %fusion.51 = f32[1,64,2,1024]{3,1,0,2:T(8,128)} fusion(bf16[1,2,1024,4096]{3,2,1,0:T(8,128)(2,1)} %param.31, f32[64,4096]{1,0:T(8,128)} %all-reduce.8.cloned.1.call-done, f32[4096]{0:T(1024)S(1)} %bitcast.559, f32[64]{0:T(128)S(1)} %copy-done.44, bf16[1,3,64,4096]{3,2,1,0:T(8,128)(2,1)} %all-gather.6.cloned.1.call-done), kind=kOutput, calls=%fused_computation.72 | convolution fusion | flops 1075052544 | bytes 18891008 | tf_op jit(solution)/shard_map/dot_general | solution.py:156
  401.7 13.0 %fusion.57 = f32[1,64,2,1024]{3,1,0,2:T(8,128)} fusion(bf16[1,2,1024,4096]{3,2,1,0:T(8,128)(2,1)} %param.31, f32[64,4096]{1,0:T(8,128)} %get-tuple-element.38, f32[64]{0:T(128)S(1)} %add_rsqrt_fusion, f32[4096]{0:T(1024)S(1)} %bitcast.560, bf16[1,3,64,4096]{3,2,1,0:T(8,128)(2,1)} %all-gather.6.cloned.1.call-done), kind=kOutput, calls=%fused_computation.74 | convolution fusion | flops 1075052544 | bytes 18891008 | tf_op jit(solution)/shard_map/dot_general | solution.py:156
  419.0 12.6 %fusion.54 = f32[1,64,2,1024]{3,1,0,2:T(8,128)} fusion(bf16[1,2,1024,4096]{3,2,1,0:T(8,128)(2,1)} %param.31, f32[64,4096]{1,0:T(8,128)} %get-tuple-element.39, f32[64]{0:T(128)S(1)} %add_rsqrt_fusion.4, f32[4096]{0:T(1024)S(1)} %bitcast.561, bf16[1,3,64,4096]{3,2,1,0:T(8,128)(2,1)} %all-gather.6.cloned.1.call-done), kind=kOutput, calls=%fused_computation.73 | convolution fusion | flops 1075052544 | bytes 18891008 | tf_op jit(solution)/shard_map/dot_general | solution.py:156
  431.6 92.2 %all-reduce.10.cloned.1.call-done = (f32[64,8192]{1,0:T(8,128)}, f32[64,8192]{1,0:T(8,128)}, f32[64,8192]{1,0:T(8,128)}) async-done(((f32[64,8192]{1,0:T(8,128)}, f32[64,8192]{1,0:T(8,128)}, f32[64,8192]{1,0:T(8,128)}), (f32[64,8192]{1,0:T(8,128)}, f32[64,8192]{1,0:T(8,128)}, f32[64,8192]{1,0:T(8,128)})) %all-reduce.10.cloned.1.call-update) | async-done | bytes 6291472 | tf_op jit(solution)/shard_map/psum | solution.py:197
  531.9 11.7 %fusion.265 = (f32[64]{0:T(128)S(1)}, f32[64,1024]{1,0:T(8,128)S(1)}) fusion(f32[2,1,64,1,1024]{4,2,3,1,0:T(8,128)} %bitcast.128, bf16[1024,8192]{1,0:T(8,128)(2,1)} %param.25, f32[64,8192]{1,0:T(8,128)} %get-tuple-element.32, f32[64]{0:T(128)S(1)} %add_rsqrt_fusion.2, f32[8192]{0:T(1024)S(1)} %copy-done.15, bf16[3,64,8192]{2,1,0:T(8,128)(2,1)S(1)} %copy-done.4), kind=kOutput, calls=%fused_computation.422 | convolution fusion | flops 1076559872 | bytes 20742912 | tf_op jit(solution)/shard_map/dot_general | solution.py:200
  548.0 12.4 %fusion.266 = (f32[64]{0:T(128)S(1)}, f32[64,1024]{1,0:T(8,128)}) fusion(f32[2,1,64,1,1024]{4,2,3,1,0:T(8,128)} %bitcast.92, bf16[1024,8192]{1,0:T(8,128)(2,1)} %param.25, f32[64,8192]{1,0:T(8,128)} %get-tuple-element.34, f32[64]{0:T(128)S(1)} %add_rsqrt_fusion.6, f32[8192]{0:T(1024)S(1)} %copy-done.15, bf16[3,64,8192]{2,1,0:T(8,128)(2,1)S(1)} %copy-done.4), kind=kOutput, calls=%fused_computation.423 | convolution fusion | flops 1076559872 | bytes 20742912 | tf_op jit(solution)/shard_map/dot_general | solution.py:200
  560.5 12.5 %fusion.267 = (f32[64]{0:T(128)S(1)}, f32[64,1024]{1,0:T(8,128)}) fusion(f32[2,1,64,1,1024]{4,2,3,1,0:T(8,128)} %bitcast.52, bf16[1024,8192]{1,0:T(8,128)(2,1)} %param.25, f32[64,8192]{1,0:T(8,128)} %get-tuple-element.33, f32[8192]{0:T(1024)S(1)} %copy-done.15, f32[64]{0:T(128)S(1)} %add_rsqrt_fusion.10, bf16[3,64,8192]{2,1,0:T(8,128)(2,1)S(1)} %copy-done.4), kind=kOutput, calls=%fused_computation.424 | convolution fusion | flops 1076559872 | bytes 20742912 | tf_op jit(solution)/shard_map/dot_general | solution.py:200
  572.9 33.0 %all-reduce.2 = (f32[64]{0:T(128)S(1)}, f32[64]{0:T(128)S(1)}, f32[64]{0:T(128)S(1)}) all-reduce(f32[64]{0:T(128)S(1)} %get-tuple-element.116, f32[64]{0:T(128)S(1)} %get-tuple-element.118, f32[64]{0:T(128)S(1)} %get-tuple-element.120), channel_id=1, replica_groups=mesh['grp'=2,'tp'=8,'dp'=2] {'grp','tp'}, use_global_device_ids=true, to_apply=%region_47.48 | all-reduce | flops 192 | bytes 1536 | tf_op jit(solution)/shard_map/pmax | solution.py:208
  608.5 29.5 %all-reduce = (f32[64]{0:T(128)S(1)}, f32[64]{0:T(128)S(1)}, f32[64]{0:T(128)S(1)}, f32[64]{0:T(128)S(1)}, f32[64]{0:T(128)S(1)}, /*index=5*/f32[64]{0:T(128)S(1)}) all-reduce(f32[64]{0:T(128)S(1)} %get-tuple-element.18, f32[64]{0:T(128)S(1)} %get-tuple-element.16, ...), channel_id=1, replica_groups=mesh['grp'=2,'tp'=8,'dp'=2] {'grp','tp'}, use_global_device_ids=true, to_apply=%region_49.50 | all-reduce | flops 384 | bytes 3072 | tf_op jit(solution)/shard_map/psum | solution.py:209
  (323 shorter events, 162.8 us)
Async XLA Ops:
  8.0 56.9 %all-gather.6.cloned.1.call-start = ((), (), s32[]{:S(2)}) async-start(), calls=%async_computation.5 | async-start | bytes 1769472 | tf_op jit(solution)/shard_map/all_gather | solution.py:96
  8.7 183.1 %all-reduce.8.cloned.1.call-start = ((), (), s32[]{:S(2)}) async-start(), calls=%async_computation.4 | async-start | bytes 2097152 | tf_op jit(solution)/shard_map/psum | solution.py:153
  52.6 73.4 %copy-start.27 = (f32[64]{0:T(128)}, f32[64]{0:T(128)S(1)}, u32[]{:S(2)}) copy-start(f32[64]{0:T(128)S(1)} %get-tuple-element.109) | copy-start | bytes 772
  52.6 73.4 %copy-start.29 = (f32[64]{0:T(128)}, f32[64]{0:T(128)S(1)}, u32[]{:S(2)}) copy-start(f32[64]{0:T(128)S(1)} %get-tuple-element.110) | copy-start | bytes 772
  52.6 73.4 %copy-start.31 = (f32[64]{0:T(128)}, f32[64]{0:T(128)S(1)}, u32[]{:S(2)}) copy-start(f32[64]{0:T(128)S(1)} %get-tuple-element.111) | copy-start | bytes 772
  53.1 13.1 %copy-start.16 = (f32[1,4096]{1,0:T(1,128)S(1)}, f32[1,4096]{1,0:T(1,128)}, u32[]{:S(2)}) copy-start(f32[1,4096]{1,0:T(1,128)} %param.26) | copy-start | bytes 49156
  87.4 8.3 %copy-start = (bf16[512,4096]{1,0:T(8,128)(2,1)S(1)}, bf16[512,4096]{1,0:T(8,128)(2,1)}, u32[]{:S(2)}) copy-start(bf16[512,4096]{1,0:T(8,128)(2,1)} %copy.297) | copy-start | bytes 12582916
  99.8 156.7 %all-gather.4.cloned.1.call-start = ((), (), s32[]{:S(2)}) async-start(), calls=%async_computation.3 | async-start | bytes 3342336 | tf_op jit(solution)/shard_map/all_gather | solution.py:95
  100.4 299.0 %all-reduce.12.cloned.1.call-start = ((), (), s32[]{:S(2)}) async-start(), calls=%async_computation.7 | async-start | bytes 4194304 | tf_op jit(solution)/shard_map/psum | solution.py:153
  126.0 68.0 %copy-start.33 = (f32[32]{0:T(128)}, f32[32]{0:T(128)S(1)}, u32[]{:S(2)}) copy-start(f32[32]{0:T(128)S(1)} %multiply_exponential_fusion.1) | copy-start | bytes 388
  194.1 26.2 %copy-start.38 = (f32[64]{0:T(128)}, f32[64]{0:T(128)S(1)}, u32[]{:S(2)}) copy-start(f32[64]{0:T(128)S(1)} %get-tuple-element.122) | copy-start | bytes 772
  236.8 11.1 %slice-start.2 = ((s8[8388608]{0:T(1024)(128)(4,1)}), s8[4194304]{0:T(1024)(128)(4,1)S(1)}, s32[]{:S(2)}) async-start(s8[8388608]{0:T(1024)(128)(4,1)} %bitcast.522), calls=%async_computation.10 | async-start | bytes 8388608
  239.5 8.4 %slice-start.3 = ((s8[8388608]{0:T(1024)(128)(4,1)}), s8[4194304]{0:T(1024)(128)(4,1)S(1)}, s32[]{:S(2)}) async-start(s8[8388608]{0:T(1024)(128)(4,1)} %bitcast.522), calls=%async_computation.11 | async-start | bytes 8388608
  256.1 267.6 %all-reduce.10.cloned.1.call-start = ((), (), s32[]{:S(2)}) async-start(), calls=%async_computation.6 | async-start | bytes 12582912 | tf_op jit(solution)/shard_map/psum | solution.py:197
  260.4 9.4 %copy-start.46 = (f32[64]{0:T(128)}, f32[64]{0:T(128)S(1)}, u32[]{:S(2)}) copy-start(f32[64]{0:T(128)S(1)} %get-tuple-element.125) | copy-start | bytes 772
  286.5 50.3 %collective-permute-start.1 = (f32[64,8,130]{2,1,0:T(8,128)}, f32[64,8,130]{2,1,0:T(8,128)}, u32[]{:S(2)}, u32[]{:S(2)}) collective-permute-start(f32[64,8,130]{2,1,0:T(8,128)} %copy.311), channel_id=1, source_target_pairs={{0,2},{2,0},{4,6},{6,4},{8,10},{10,8},{12,14},{14,12},{1,3},{3,1},... | collective-permute-start | bytes 798728 | tf_op jit(solution)/shard_map/ppermute | solution.py:18
  288.6 9.2 %copy-start.22 = (f32[64,32]{0,1:T(8,128)S(1)}, f32[64,32]{0,1:T(8,128)}, u32[]{:S(2)}) copy-start(f32[64,32]{0,1:T(8,128)} %get-tuple-element.95) | copy-start | bytes 24580
  288.6 9.2 %copy-start.23 = (f32[64,32]{0,1:T(8,128)S(1)}, f32[64,32]{0,1:T(8,128)}, u32[]{:S(2)}) copy-start(f32[64,32]{0,1:T(8,128)} %get-tuple-element.96) | copy-start | bytes 24580
  305.5 9.7 %copy-start.20 = (f32[64,32]{0,1:T(8,128)S(1)}, f32[64,32]{0,1:T(8,128)}, u32[]{:S(2)}) copy-start(f32[64,32]{0,1:T(8,128)} %get-tuple-element.107) | copy-start | bytes 24580
  305.5 9.7 %copy-start.21 = (f32[64,32]{0,1:T(8,128)S(1)}, f32[64,32]{0,1:T(8,128)}, u32[]{:S(2)}) copy-start(f32[64,32]{0,1:T(8,128)} %get-tuple-element.108) | copy-start | bytes 24580
  305.5 27.0 %collective-permute-start = (f32[64,8,129]{2,1,0:T(8,128)}, f32[64,8,129]{2,1,0:T(8,128)}, u32[]{:S(2)}, u32[]{:S(2)}) collective-permute-start(f32[64,8,129]{2,1,0:T(8,128)} %copy.282), channel_id=1, source_target_pairs={{0,2},{2,0},{4,6},{6,4},{8,10},{10,8},{12,14},{14,12},{1,3},{3,1},... | collective-permute-start | bytes 792584 | tf_op jit(solution)/shard_map/ppermute | solution.py:18
  321.4 8.3 %copy-start.51 = (f32[8192]{0:T(1024)S(1)}, f32[8192]{0:T(1024)}, u32[]{:S(2)}) copy-start(f32[8192]{0:T(1024)} %param.19) | copy-start | bytes 98308
  321.4 8.3 %copy-start.53 = (f32[64]{0:T(128)S(1)}, f32[64]{0:T(128)}, u32[]{:S(2)}) copy-start(f32[64]{0:T(128)} %copy-done.52) | copy-start | bytes 772
  326.5 17.8 %collective-permute-start.2 = (f32[64,8,131]{2,1,0:T(8,128)}, f32[64,8,131]{2,1,0:T(8,128)}, u32[]{:S(2)}, u32[]{:S(2)}) collective-permute-start(f32[64,8,131]{2,1,0:T(8,128)} %copy.333), channel_id=1, source_target_pairs={{0,2},{2,0},{4,6},{6,4},{8,10},{10,8},{12,14},{14,12},{1,3},{3,1},... | collective-permute-start | bytes 804872 | tf_op jit(solution)/shard_map/ppermute | solution.py:18
  330.8 8.5 %copy-start.19 = (f32[64,8,2]{0,1,2:T(8,128)S(1)}, f32[64,8,2]{0,1,2:T(8,128)}, u32[]{:S(2)}) copy-start(f32[64,8,2]{0,1,2:T(8,128)} %copy.310) | copy-start | bytes 12292
  369.8 13.0 %slice-start = ((s8[8388608]{0:T(1024)(128)(4,1)}), s8[4194304]{0:T(1024)(128)(4,1)S(1)}, s32[]{:S(2)}) async-start(s8[8388608]{0:T(1024)(128)(4,1)} %bitcast.518), calls=%async_computation.8 | async-start | bytes 8388608
  414.7 112.9 %all-to-all-start.2 = ((f32[1,64,2,1024]{3,1,0,2:T(8,128)}), f32[1,64,2,1024]{3,1,0,2:T(8,128)}, u32[]{:S(2)}, u32[]{:S(2)}) async-start(f32[1,64,2,1024]{3,1,0,2:T(8,128)} %fusion.57), calls=%async_computation.2 | async-start | bytes 1048576 | tf_op jit(solution)/shard_map/all_to_all | solution.py:160
  527.6 16.0 %all-to-all-start.1 = ((f32[1,64,2,1024]{3,1,0,2:T(8,128)}), f32[1,64,2,1024]{3,1,0,2:T(8,128)}, u32[]{:S(2)}, u32[]{:S(2)}) async-start(f32[1,64,2,1024]{3,1,0,2:T(8,128)} %fusion.54), calls=%async_computation.1 | async-start | bytes 1048576 | tf_op jit(solution)/shard_map/all_to_all | solution.py:160
  543.6 16.8 %all-to-all-start = ((f32[1,64,2,1024]{3,1,0,2:T(8,128)}), f32[1,64,2,1024]{3,1,0,2:T(8,128)}, u32[]{:S(2)}, u32[]{:S(2)}) async-start(f32[1,64,2,1024]{3,1,0,2:T(8,128)} %fusion.51), calls=%async_computation | async-start | bytes 1048576 | tf_op jit(solution)/shard_map/all_to_all | solution.py:160
  560.5 45.5 %copy-start.37 = (s32[64]{0:T(128)S(1)}, s32[64]{0:T(128)}, u32[]{:S(2)}) copy-start(s32[64]{0:T(128)} %get-tuple-element.87) | copy-start | bytes 772
  560.5 45.7 %copy-start.36 = (s32[64]{0:T(128)S(1)}, s32[64]{0:T(128)}, u32[]{:S(2)}) copy-start(s32[64]{0:T(128)} %get-tuple-element.88) | copy-start | bytes 772
  560.5 46.9 %copy-start.35 = (s32[64]{0:T(128)S(1)}, s32[64]{0:T(128)}, u32[]{:S(2)}) copy-start(s32[64]{0:T(128)} %get-tuple-element.86) | copy-start | bytes 772
  (37 other events, 150.3 us)
Sparse Core Ops, SparseCore 0:
  10.8 47.1 all-gather.5
  100.0 91.8 all-reduce.7
  256.2 104.6 all-reduce.11
  385.8 137.9 all-reduce.9
Sparse Core Ops, SparseCore 1:
  102.4 52.9 all-gather.3
where the time goes:
time: 661 us; the launch traced here: 649 us
  matrix products  234 us (35%)
  waiting for transfers between devices  158 us (24%)
  local copies, waits for them, and re-layouts  117 us (18%)
  blocking collectives  62.5 us (9%)
  other arithmetic  43.5 us (7%)
  starting transfers between devices  16.8 us (3%)
  between operations  16.8 us (3%)
    psum x1, waiting for transfers between devices, body(): mixed_sum = lax.psum(partial_value, ('grp', 'tp'))  92.2 us
    psum x2, waiting for transfers between devices, body(): small_mixed = lax.psum(small_partial, 'tp')  61.5 us
    dot_general x3, matrix products, body(): lax.dot_general(small_final, small_table, (((1,), (1,)), ((), ())), prefe...  38.7 us
    dot_general x3, matrix products, body(): lax.dot_general(final_rows, base_unembed, (((1,), (1,)), ((), ())), prefe...  36.6 us
    pmax x1, blocking collectives, body(): row_max = lax.pmax(local_max, ('grp', 'tp'))  33 us
    psum x1, blocking collectives, body(): lax.psum((jnp.sum(jnp.exp(steered - row_max[:, None]), axis=-1), picked_l...  29.5 us
    dot_general x3, matrix products, body(): jnp.dot(normed, base_query, preferred_element_type=jnp.float32)  27.6 us
    dot_general x2, local copies, waits for them, and re-layouts, body(): jnp.dot(normed, base_query, preferred_element_type=jnp.float32)  25.5 us
  transfers between devices with their start and end apart: 11, of which 3 were waited for; matrix products, arithmetic and copies ran while one was open for 52% of the time, Pallas kernels for 0%

commit v1 on v0

v1 whole, which is shorter than its diff:
```python
import functools
import math

import jax
import jax.numpy as jnp
from jax import lax
from jax.experimental import pallas as pl
from jax.experimental.pallas import tpu as pltpu
from jax.sharding import PartitionSpec as P

HD = 128
STEPS = 3
CACHE = 128


EPSILON = 1e-05
NEGATIVE = -1e30
VMEM_LIMIT = 48 * 1024 * 1024


def partner(array, axis, bit):
    return lax.ppermute(array, axis, [(i, i ^ 1 << bit) for i in range(lax.axis_size(axis))])


def tile_of(size, most):
    tile = min(size, most)
    while size % tile:
        tile //= 2
    return tile


def rotation_tables(positions, first_pair, width, head_size):
    pair_index = (first_pair + jnp.arange(width) // 2).astype(jnp.float32)
    frequency = jnp.exp(pair_index * (-2.0 * math.log(10000.0) / head_size))
    angles = positions.astype(jnp.float32)[:, None] * frequency[None, :]
    sign = jnp.where(jnp.arange(width) % 2 == 0, -1.0, 1.0)
    return jnp.cos(angles), jnp.sin(angles) * sign


def rotate(values, cosine, sine):
    copies = values.shape[1] // cosine.shape[1]
    cosine = jnp.tile(cosine, (1, copies))
    sine = jnp.tile(sine, (1, copies))
    even = (jnp.arange(values.shape[1]) % 2 == 0)[None, :]
    other = jnp.where(even, jnp.roll(values, -1, axis=1), jnp.roll(values, 1, axis=1))
    return (values * cosine + other * sine).astype(jnp.bfloat16)


def norm_rows(values, gain_row):
    values = values.astype(jnp.float32)
    scaling = lax.rsqrt(jnp.mean(values * values, axis=-1, keepdims=True) + EPSILON)
    return (values * scaling * gain_row).astype(jnp.bfloat16)


def project_kernel(tile, weight_count, x_ref, gain_ref, *refs):
    weights = refs[:weight_count]
    outs = refs[weight_count:-1]
    scale_ref = refs[-1]
    step = pl.program_id(0)
    rows, depth = x_ref.shape

    @pl.when(step == 0)
    def _():
        def add(index, total):
            part = x_ref[:, pl.ds(pl.multiple_of(index * tile, tile), tile)].astype(jnp.float32)
            return total + jnp.sum(part * part, axis=-1, keepdims=True)

        total = lax.fori_loop(0, depth // tile, add, jnp.zeros((rows, 1), jnp.float32))
        scaling = lax.rsqrt(total / depth + EPSILON)
        scale_ref[...] = jnp.broadcast_to(scaling, scale_ref.shape)
        for out in outs:
            out[...] = jnp.zeros_like(out)

    columns = pl.ds(pl.multiple_of(step * tile, tile), tile)
    normed = x_ref[:, columns].astype(jnp.float32) * scale_ref[:, :1] * gain_ref[:, columns]
    normed = normed.astype(jnp.bfloat16)
    place = 0
    for weight in weights:
        if len(weight.shape) == 2:
            outs[place][...] += jnp.dot(normed, weight[...], preferred_element_type=jnp.float32)
            place += 1
        else:
            for index in range(weight.shape[0]):
                outs[place][...] += jnp.dot(
                    normed, weight[index], preferred_element_type=jnp.float32
                )
                place += 1


def project(x, gain, weights, tile):
    rows, depth = x.shape
    tile = tile_of(depth, tile)
    specs = []
    shapes = []
    for weight in weights:
        width = weight.shape[-1]
        if weight.ndim == 2:
            specs.append(pl.BlockSpec((tile, width), lambda k: (k, 0)))
            shapes.append((rows, width))
        else:
            specs.append(pl.BlockSpec((weight.shape[0], tile, width), lambda k: (0, k, 0)))
            shapes.extend([(rows, width)] * weight.shape[0])
    return pl.pallas_call(
        functools.partial(project_kernel, tile, len(weights)),
        grid=(depth // tile,),
        in_specs=[
            pl.BlockSpec((rows, depth), lambda k: (0, 0)),
            pl.BlockSpec((1, depth), lambda k: (0, 0)),
        ]
        + specs,
        out_specs=[pl.BlockSpec(shape, lambda k: (0, 0)) for shape in shapes],
        out_shape=[jax.ShapeDtypeStruct(shape, jnp.float32) for shape in shapes],
        scratch_shapes=[pltpu.VMEM((rows, 128), jnp.float32)],
        compiler_params=pltpu.CompilerParams(vmem_limit_bytes=VMEM_LIMIT),
    )(x, gain, *weights)


def out_kernel(x_ref, w_ref, o_ref):
    o_ref[...] = jnp.dot(x_ref[...], w_ref[...], preferred_element_type=jnp.float32).astype(
        o_ref.dtype
    )


def out_project(x, weight, most):
    rows, depth = x.shape
    width = weight.shape[1]
    tile = tile_of(width, most)
    return pl.pallas_call(
        out_kernel,
        grid=(width // tile,),
        in_specs=[
            pl.BlockSpec((rows, depth), lambda n: (0, 0)),
            pl.BlockSpec((depth, tile), lambda n: (0, n)),
        ],
        out_specs=pl.BlockSpec((rows, tile), lambda n: (0, n)),
        out_shape=jax.ShapeDtypeStruct((rows, width), jnp.bfloat16),
        compiler_params=pltpu.CompilerParams(vmem_limit_bytes=VMEM_LIMIT),
    )(x, weight)


def logit_kernel(x_ref, w_ref, o_ref):
    o_ref[...] = lax.dot_general(
        x_ref[...], w_ref[...], (((1,), (1,)), ((), ())), preferred_element_type=jnp.float32
    )


def logit_project(x, table, most):
    rows, depth = x.shape
    parts, width = table.shape[:2]
    tile = tile_of(width, most)
    return pl.pallas_call(
        logit_kernel,
        grid=(parts, width // tile),
        in_specs=[
            pl.BlockSpec((rows, depth), lambda p, n: (0, 0)),
            pl.BlockSpec((None, tile, depth), lambda p, n: (p, n, 0)),
        ],
        out_specs=pl.BlockSpec((None, rows, tile), lambda p, n: (p, 0, n)),
        out_shape=jax.ShapeDtypeStruct((parts, rows, width), jnp.float32),
        compiler_params=pltpu.CompilerParams(vmem_limit_bytes=VMEM_LIMIT),
    )(x, table)


def attention_weights(cached_scores, fresh_scores, visible, causal):
    factor = 1.0 / math.sqrt(HD)
    cached_scores = jnp.where(visible, cached_scores * factor, NEGATIVE)
    fresh_scores = jnp.where(causal, fresh_scores * factor, NEGATIVE)
    row_max = jnp.maximum(
        jnp.max(cached_scores, axis=-1, keepdims=True),
        jnp.max(fresh_scores, axis=-1, keepdims=True),
    )
    cached_exp = jnp.exp(cached_scores - row_max)
    fresh_exp = jnp.exp(fresh_scores - row_max)
    totals = jnp.sum(cached_exp, axis=-1, keepdims=True) + jnp.sum(
        fresh_exp, axis=-1, keepdims=True
    )
    return ((cached_exp / totals).astype(jnp.bfloat16), (fresh_exp / totals).astype(jnp.bfloat16))


def mix_rows(partial, inputs, gain, axes):
    count = lax.axis_size(axes)
    rows = partial.shape[0] // count
    mixed = lax.psum_scatter(
        partial.reshape(count, rows, partial.shape[1]), axes, scatter_dimension=0, tiled=False
    )
    start = lax.axis_index(axes) * rows
    hidden = lax.dynamic_slice_in_dim(inputs, start, rows, 0).astype(jnp.float32) + mixed.astype(
        jnp.float32
    )
    final = norm_rows(hidden, gain)
    return lax.all_gather(final, axes, axis=0, tiled=False).reshape(partial.shape)


def body(
    base_inputs,
    small_inputs,
    base_norm_gain,
    base_query,
    base_keys_values,
    base_output,
    base_cache,
    base_final_gain,
    base_unembed,
    small_norm_gain,
    small_projections,
    small_output,
    small_cache,
    small_final_gain,
    small_unembed,
    lengths,
    next_tokens,
):
    row_count = lengths.shape[0]
    total_rows = STEPS * row_count
    slice_width = base_keys_values.shape[2]
    share_count = HD // slice_width
    group_size = base_query.shape[1] // slice_width
    slice_index = lax.axis_index("tp") % share_count
    first_pair = slice_index * (slice_width // 2)
    block_index = lax.axis_index(("grp", "tp"))
    vocab_width = base_unembed.shape[0]
    small_heads = small_projections.shape[3] // HD
    every = ("grp", "tp")
    small_full = lax.all_gather(small_inputs[0], "tp", axis=2, tiled=True)
    small_full = small_full.reshape(total_rows, -1)
    base_full = lax.all_gather(base_inputs, every, axis=2, tiled=True).reshape(total_rows, -1)
    positions = (jnp.arange(STEPS)[:, None] + lengths[None, :]).reshape(-1)
    visible = (jnp.arange(CACHE)[None, :] < lengths[:, None])[:, None, None, :]
    step_range = jnp.arange(STEPS)
    causal = step_range[None, :] <= step_range[:, None]

    small_q, small_k, small_v = project(
        small_full, small_norm_gain, [small_projections[0]], 512
    )
    cosine, sine = rotation_tables(positions, 0, HD, HD)
    by_head = (STEPS, row_count, small_heads, HD)
    small_q = rotate(small_q, cosine, sine).reshape(by_head)
    small_k = rotate(small_k, cosine, sine).reshape(by_head)
    small_v = small_v.astype(jnp.bfloat16).reshape(by_head)
    keys = small_cache[0, 0].reshape(row_count, small_heads, HD, CACHE)
    values = small_cache[0, 1].reshape(row_count, small_heads, HD, CACHE)
    cached = jnp.einsum("srhd,rhdl->rhsl", small_q, keys, preferred_element_type=jnp.float32)
    fresh = jnp.einsum("srhd,nrhd->rhsn", small_q, small_k, preferred_element_type=jnp.float32)
    cached, fresh = attention_weights(cached, fresh, visible, causal[None, None])
    heads = jnp.einsum("rhsl,rhdl->srhd", cached, values, preferred_element_type=jnp.float32)
    heads = heads + jnp.einsum(
        "rhsn,nrhd->srhd", fresh, small_v, preferred_element_type=jnp.float32
    )
    heads = heads.astype(jnp.bfloat16).reshape(total_rows, small_heads * HD)
    small_partial = out_project(heads, small_output[0], 1024)
    small_final = mix_rows(small_partial, small_full, small_final_gain[0], "tp")
    small_logits = logit_project(small_final, small_unembed[0], 512)
    group = lax.axis_index("grp")
    own = lax.dynamic_index_in_dim(small_logits, group, 0, keepdims=False)
    theirs = lax.dynamic_index_in_dim(small_logits, 1 - group, 0, keepdims=False)
    received = lax.ppermute(theirs, "grp", [(0, 1), (1, 0)])

    query, new_key, new_value = project(
        base_full, base_norm_gain[None], [base_query, base_keys_values], 1024
    )
    cosine, sine = rotation_tables(positions, first_pair, slice_width, HD)
    query = rotate(query, cosine, sine).reshape(STEPS, row_count, group_size, slice_width)
    new_key = rotate(new_key, cosine, sine).reshape(STEPS, row_count, slice_width)
    new_value = new_value.astype(jnp.bfloat16).reshape(STEPS, row_count, slice_width)
    cached = jnp.einsum("srgd,rdl->rsgl", query, base_cache[0], preferred_element_type=jnp.float32)
    fresh = jnp.einsum("srgd,nrd->rsgn", query, new_key, preferred_element_type=jnp.float32)
    for bit in range(share_count.bit_length() - 1):
        cached = cached + partner(cached, "tp", bit)
        fresh_flat = fresh.reshape(row_count, -1)
        fresh = fresh + partner(fresh_flat, "tp", bit).reshape(fresh.shape)
    cached, fresh = attention_weights(cached, fresh, visible, causal[:, None, :][None])
    heads = jnp.einsum("rsgl,rdl->srgd", cached, base_cache[1], preferred_element_type=jnp.float32)
    heads = heads + jnp.einsum(
        "rsgn,nrd->srgd", fresh, new_value, preferred_element_type=jnp.float32
    )
    heads = heads.astype(jnp.bfloat16).reshape(total_rows, group_size * slice_width)
    partial = out_project(heads, base_output, 1024)
    final_rows = mix_rows(partial, base_full, base_final_gain, every)
    base_logits = logit_project(final_rows, base_unembed[None], 256)[0]
    gap = jnp.where(group == 0, own - received, received - own)
    steered = base_logits + gap

    local_max = jnp.max(steered, axis=-1)
    local_total = jnp.sum(jnp.exp(steered - local_max[:, None]), axis=-1)
    token_local = next_tokens.reshape(-1) - block_index * vocab_width
    token_hit = jnp.arange(vocab_width)[None, :] == token_local[:, None]
    picked = jnp.sum(jnp.where(token_hit, steered, 0.0), axis=-1)
    stats = lax.all_gather(jnp.stack([local_max, local_total, picked]), every, axis=0)
    row_max = jnp.max(stats[:, 0], axis=0)
    exp_total = jnp.sum(stats[:, 1] * jnp.exp(stats[:, 0] - row_max[None]), axis=0)
    log_norm = row_max + jnp.log(exp_total)
    chosen = jnp.sum(stats[:, 2], axis=0) - log_norm
    log_probs = steered - log_norm[:, None]
    return (
        log_probs.reshape(STEPS, row_count, vocab_width),
        jnp.sum(chosen.reshape(STEPS, row_count), axis=0),
    )


def solution(mesh):
    placed = (
        P(None, "dp", ("grp", "tp")),
        P("grp", None, "dp", "tp"),
        P(),
        P(None, ("grp", "tp")),
        P(None, None, ("grp", "tp")),
        P(("grp", "tp"), None),
        P(None, "dp", ("grp", "tp"), None),
        P(),
        P(("grp", "tp"), None),
        P("grp", None),
        P("grp", None, None, "tp"),
        P("grp", "tp", None),
        P("grp", None, "dp", "tp", None),
        P("grp", None),
        P("grp", None, "tp", None),
        P("dp"),
        P(None, "dp"),
    )
    return jax.shard_map(
        body,
        mesh=mesh,
        in_specs=placed,
        out_specs=(P(None, "dp", ("grp", "tp")), P("dp")),
        check_vma=False,
    )
```

time: 661 us -> 398 us (0.60); the launches traced: 649 us -> 397 us
  matrix products: 234 us -> 18.7 us
  local copies, waits for them, and re-layouts: 117 us -> 33.3 us
  waiting for transfers between devices: 158 us -> 234 us
  Pallas kernels: 0 us -> 49 us
  blocking collectives: 62.5 us -> 30.4 us
  other arithmetic: 43.5 us -> 14.9 us
  starting transfers between devices: 16.8 us -> 2.58 us
    dot_general x48 -> x8, matrix products: 234 us -> 18.7 us  [the longest x1 8.01 us: body(): jnp.einsum('rhsl,rhdl->srhd', cached, values, preferred_element_type=jnp....]
    psum x3 -> x0, waiting for transfers between devices: 154 us -> none  [the longest x1 92.2 us: body(): mixed_sum = lax.psum(partial_value, ('grp', 'tp'))]
    all_gather x1 -> x3, waiting for transfers between devices: 0.03 us -> 94.5 us  [the longest x2 80.4 us: mix_rows(): lax.all_gather(final, axes, axis=0, tiled=False).reshape(partial.shape)]
    reduce_scatter x0 -> x2, waiting for transfers between devices: none -> 85.2 us  [mix_rows(): lax.psum_scatter(partial.reshape(count, rows, partial.shape[1]), axes, sc...]
    dot_general x15 -> x2, local copies, waits for them, and re-layouts: 76.9 us -> 0.39 us  [the longest x1 0.23 us: body(): jnp.einsum('srhd,nrhd->rhsn', small_q, small_k, preferred_element_type=jn...]
    pallas_call x0 -> x6, Pallas kernels: none -> 49 us  [the longest x2 20.1 us: project(): pl.pallas_call(functools.partial(project_kernel, tile, len(weights)), gri...]
    pmax x1 -> x0, blocking collectives: 33 us -> none  [body(): row_max = lax.pmax(local_max, ('grp', 'tp'))]
    all_gather x1, waiting for transfers between devices: 0.02 us -> 30.7 us  [body(): small_full = lax.all_gather(small_inputs[0], 'tp', axis=2, tiled=True)]
  transfers between devices with their start and end apart: 11 -> 9, of which waited for: 3 -> 7; matrix products, arithmetic and copies ran while one was open for 52% -> 14% of each run, Pallas kernels for 0% -> 12%
where the time goes in v1:
time: 398 us; the launch traced here: 397 us
  waiting for transfers between devices  234 us (59%)
  Pallas kernels  49 us (12%)
  local copies, waits for them, and re-layouts  33.3 us (8%)
  blocking collectives  30.4 us (8%)
  matrix products  18.7 us (5%)
  other arithmetic  14.9 us (4%)
  between operations  14.6 us (4%)
    reduce_scatter x2, waiting for transfers between devices, mix_rows(): lax.psum_scatter(partial.reshape(count, rows, partial.shape[1]), axes, sc...  85.2 us
    all_gather x2, waiting for transfers between devices, mix_rows(): lax.all_gather(final, axes, axis=0, tiled=False).reshape(partial.shape)  80.4 us
    all_gather x1, waiting for transfers between devices, body(): small_full = lax.all_gather(small_inputs[0], 'tp', axis=2, tiled=True)  30.7 us
    all_gather x1, blocking collectives, body(): lax.all_gather(jnp.stack([local_max, local_total, picked]), every, axis=0)  30.4 us
    ppermute x2, waiting for transfers between devices, partner(): lax.ppermute(array, axis, [(i, i ^ 1 << bit) for i in range(lax.axis_size...  22.1 us
    pallas_call x2, Pallas kernels, project(): pl.pallas_call(functools.partial(project_kernel, tile, len(weights)), gri...  20.1 us
    pallas_call x2, Pallas kernels, logit_project(): pl.pallas_call(logit_kernel, grid=(parts, width // tile), in_specs=[pl.Bl...  18.7 us
    all_gather x1, waiting for transfers between devices, body(): lax.all_gather(base_inputs, every, axis=2, tiled=True)  14.1 us
  transfers between devices with their start and end apart: 9, of which 7 were waited for; matrix products, arithmetic and copies ran while one was open for 14% of the time, Pallas kernels for 12%

profile of v1, /device:TPU:0, one launch (start us, length us, event | category | flops | bytes accessed | tf_op | source)
XLA Modules:
  0.0 397.4 jit_solution(17926382412250540778)
XLA Ops:
  9.5 4.8 %copy.137.refs_1_ = bf16[2,8192,64]{2,1,0:T(8,128)(2,1)} copy(bf16[2,8192,64]{1,2,0:T(8,128)(2,1)} %param.21) | data formatting | bytes 4194304 | tf_op args[4]
  14.8 11.6 %fusion.67 = (bf16[1,1,64,512,128]{4,3,2,1,0:T(8,128)(2,1)}, bf16[1,1,64,512,128]{4,3,2,1,0:T(8,128)(2,1)}) fusion(bf16[1,2,64,512,128]{4,3,2,1,0:T(8,128)(2,1)} %param.29), kind=kLoop, calls=%fused_computation.133 | loop fusion | bytes 33554432 | tf_op jit(solution)/shard_map/slice | solution.py:241
  26.5 30.7 %all-gather.13.cloned.1.call-done = bf16[1,3,64,4096]{3,2,1,0:T(8,128)(2,1)} async-done(((bf16[1,3,64,512]{3,2,1,0:T(8,128)(2,1)}), bf16[1,3,64,4096]{3,2,1,0:T(8,128)(2,1)}) %all-gather.13.cloned.1.call-update) | async-done | bytes 1572880 | tf_op jit(solution)/shard_map/all_gather | solution.py:224
  57.2 1.4 copy-done.4
  58.6 9.7 %shard_map.179 = (f32[192,512]{1,0:T(8,128)S(1)}, f32[192,512]{1,0:T(8,128)S(1)}, f32[192,512]{1,0:T(8,128)S(1)}) custom-call(bf16[192,4096]{1,0:T(8,128)(2,1)S(1)} %bitcast.130, f32[1,4096]{1,0:T(1,128)S(1)} %copy-done.7, bf16[3,4096,512]{2,1,0:T(8,128)(2,1)} %bitcast.136), custom_call_target="tpu_custom_call" | custom-call | tf_op jit(solution)/shard_map/pallas_call | solution.py:103
  70.3 5.8 %fusion.77 = (f32[64,4,3]{2,1,0:T(4,128)S(1)}, f32[64,4,3,128]{3,2,1,0:T(4,128)S(1)}) fusion(bf16[64,4,128,128]{3,2,1,0:T(8,128)(2,1)} %bitcast.133, bf16[3,64,4,128]{3,2,1,0:T(4,128)(2,1)S(1)} %reshape.405, pred[64,128]{1,0:T(8,128)(4,1)S(1)} %iota_compare_fusion.1), kind=kOutput, calls=%fused_computation.143 | convolution fusion | flops 25459968 | bytes 8989696 | tf_op jit(solution)/shard_map/srhd,rhdl->rhsl/dot_general | solution.py:242
  78.4 8.0 %fusion.4 = bf16[3,64,4,128]{3,0,2,1:T(4,128)(2,1)S(1)} fusion(f32[3,64,4,128]{3,0,2,1:T(4,128)S(1)} %convolution_bitcast_fusion.2, bf16[64,4,128,128]{3,2,1,0:T(8,128)(2,1)} %bitcast.137, f32[64,4,3,128]{3,2,1,0:T(4,128)S(1)} %get-tuple-element.56, f32[64,4,3]{2,1,0:T(4,128)S(1)} %add.206, f32[64,4,3]{2,1,0:T(4,128)S(1)} %max.17), kind=kOutput, calls=%fused_computation.9 | convolution fusion | flops 25657344 | bytes 9377792 | tf_op jit(solution)/shard_map/rhsl,rhdl->srhd/dot_general | solution.py:245
  86.5 2.9 shard_map.180
  89.7 14.1 %all-gather.11.cloned.1.call-done = bf16[3,64,8192]{2,1,0:T(8,128)(2,1)} async-done(((bf16[3,64,512]{2,1,0:T(8,128)(2,1)}), bf16[3,64,8192]{2,1,0:T(8,128)(2,1)}) %all-gather.11.cloned.1.call-update) | async-done | bytes 3145744 | tf_op jit(solution)/shard_map/all_gather | solution.py:226
  103.8 1.9 copy-done.2
  105.7 10.4 %shard_map.176 = (f32[192,512]{1,0:T(8,128)S(1)}, f32[192,64]{1,0:T(8,128)S(1)}, f32[192,64]{1,0:T(8,128)S(1)}) custom-call(bf16[192,8192]{1,0:T(8,128)(2,1)S(1)} %bitcast.126, f32[1,8192]{1,0:T(1,128)S(1)} %bitcast.132, bf16[8192,512]{1,0:T(8,128)(2,1)} %refs_0_.1, bf16[2,8192,64]{2,1,0:T(8,128)(2,1)} %copy.137.refs_1_), custom_call_target="tpu_custom_call" | custom-call | tf_op jit(solution)/shard_map/pallas_call | solution.py:103
  118.0 1.6 fusion.6
  119.6 1.4 collective-permute-start
  121.0 1.3 fusion.23
  123.3 22.1 %collective-permute-done.1 = f32[64,72]{0,1:T(8,128)S(1)} collective-permute-done((f32[64,72]{0,1:T(8,128)S(1)}, f32[64,72]{0,1:T(8,128)S(1)}, u32[]{:S(2)}, u32[]{:S(2)}) %collective-permute-start.1) | collective-permute-done | bytes 18464 | tf_op jit(solution)/shard_map/ppermute | solution.py:22
  149.1 7.2 %shard_map.177 = bf16[192,8192]{1,0:T(8,128)(2,1)S(1)} custom-call(bf16[192,512]{1,0:T(8,128)(2,1)S(1)} %reshape.401.x_ref, bf16[512,8192]{1,0:T(8,128)(2,1)} %w_ref.1), custom_call_target="tpu_custom_call" | custom-call | tf_op jit(solution)/shard_map/pallas_call | solution.py:128
  156.3 2.7 reshape.402
  159.1 12.9 %reduce-scatter.5.cloned.1.call-done = bf16[1,24,4096]{2,1,0:T(8,128)(2,1)} async-done(((bf16[8,24,4096]{2,1,0:T(8,128)(2,1)}), bf16[1,24,4096]{2,1,0:T(8,128)(2,1)}) %reduce-scatter.5.cloned.1.call-update) | async-done | bytes 196624 | tf_op jit(solution)/shard_map/reduce_scatter | solution.py:183
  172.0 1.2 multiply_reduce_fusion.1
  173.2 1.8 multiply_convert_fusion.1
  175.1 72.3 %reduce-scatter.3.cloned.1.call-done = bf16[1,12,8192]{2,1,0:T(8,128)(2,1)} async-done(((bf16[16,12,8192]{2,1,0:T(8,128)(2,1)}), bf16[1,12,8192]{2,1,0:T(8,128)(2,1)}) %reduce-scatter.3.cloned.1.call-update) | async-done | bytes 196624 | tf_op jit(solution)/shard_map/reduce_scatter | solution.py:183
  247.4 1.3 multiply_reduce_fusion
  248.7 1.9 fusion.27
  250.7 42.6 %all-gather.15.cloned.1.call-done.x_ref = bf16[192,4096]{1,0:T(8,128)(2,1)} async-done(((bf16[24,4096]{1,0:T(8,128)(2,1)}), bf16[192,4096]{1,0:T(8,128)(2,1)}) %all-gather.15.cloned.1.call-update) | async-done | bytes 1572880 | tf_op jit(solution)/shard_map/all_gather | solution.py:191
  293.3 1.4 copy-done.5
  294.7 9.4 %shard_map.181 = f32[2,192,1024]{2,1,0:T(8,128)S(1)} custom-call(bf16[192,4096]{1,0:T(8,128)(2,1)S(1)} %copy-done.5, bf16[2,1024,4096]{2,1,0:T(8,128)(2,1)} %bitcast.135), custom_call_target="tpu_custom_call" | custom-call | tf_op jit(solution)/shard_map/pallas_call | solution.py:151
  304.1 1.2 copy-done
  306.3 37.8 %all-gather.17.cloned.1.call-done = bf16[16,12,8192]{2,1,0:T(8,128)(2,1)} async-done(((bf16[1,12,8192]{2,1,0:T(8,128)(2,1)}), bf16[16,12,8192]{2,1,0:T(8,128)(2,1)}) %all-gather.17.cloned.1.call-update) | async-done | bytes 3145744 | tf_op jit(solution)/shard_map/all_gather | solution.py:191
  344.1 3.2 reshape.422.x_ref
  347.3 9.3 %shard_map.178 = f32[1,192,1024]{2,1,0:T(8,128)S(1)} custom-call(bf16[192,8192]{1,0:T(8,128)(2,1)S(1)} %reshape.422.x_ref, bf16[1,1024,8192]{2,1,0:T(8,128)(2,1)} %bitcast.134), custom_call_target="tpu_custom_call" | custom-call | tf_op jit(solution)/shard_map/pallas_call | solution.py:151
  356.7 1.4 fusion.63
  358.4 30.4 %all-gather.5 = f32[16,3,192]{2,1,0:T(4,128)S(1)} all-gather(f32[1,3,192]{2,1,0:T(4,128)S(1)} %maximum_bitcast_fusion), channel_id=5, replica_groups=mesh['grp'=2,'tp'=8,'dp'=2] {'grp','tp'}, dimensions={0}, use_global_device_ids=true | all-gather | bytes 39168 | tf_op jit(solution)/shard_map/all_gather | solution.py:288
  (112 shorter events, 16.9 us)
Async XLA Ops:
  7.2 7.1 %copy-start.11 = (s32[64]{0:T(128)S(1)}, s32[64]{0:T(128)}, u32[]{:S(2)}) copy-start(s32[64]{0:T(128)} %param.32) | copy-start | bytes 772
  7.2 50.0 %all-gather.13.cloned.1.call-start = ((), (), s32[]{:S(2)}) async-start(), calls=%async_computation.5 | async-start | bytes 1769472 | tf_op jit(solution)/shard_map/all_gather | solution.py:224
  7.9 95.9 %all-gather.11.cloned.1.call-start = ((), (), s32[]{:S(2)}) async-start(), calls=%async_computation.2 | async-start | bytes 3342336 | tf_op jit(solution)/shard_map/all_gather | solution.py:226
  8.7 163.4 %reduce-scatter.5.cloned.1.call-start = ((), (), s32[]{:S(2)}) async-start(), calls=%async_computation.4 | async-start | bytes 1769472 | tf_op jit(solution)/shard_map/reduce_scatter | solution.py:183
  14.8 42.4 %copy-start.7 = (f32[1,4096]{1,0:T(1,128)S(1)}, f32[1,4096]{1,0:T(1,128)}, u32[]{:S(2)}) copy-start(f32[1,4096]{1,0:T(1,128)} %gain_ref.1) | copy-start | bytes 49156
  57.2 1.4 copy-start.4
  78.3 8.2 %copy-start.3 = (bf16[1,512,4096]{2,1,0:T(8,128)(2,1)S(1)}, bf16[1,512,4096]{2,1,0:T(8,128)(2,1)}, u32[]{:S(2)}) copy-start(bf16[1,512,4096]{2,1,0:T(8,128)(2,1)} %param.28) | copy-start | bytes 12582916
  86.4 17.4 %copy-start.6 = (f32[8192]{0:T(1024)S(1)}, f32[8192]{0:T(1024)}, u32[]{:S(2)}) copy-start(f32[8192]{0:T(1024)} %param.19) | copy-start | bytes 98308
  89.5 157.9 %reduce-scatter.3.cloned.1.call-start = ((), (), s32[]{:S(2)}) async-start(), calls=%async_computation.3 | async-start | bytes 4456448 | tf_op jit(solution)/shard_map/reduce_scatter | solution.py:183
  103.8 1.9 copy-start.2
  119.6 26.5 %collective-permute-start = (f32[64,3,8,128]{3,2,1,0:T(8,128)S(1)}, f32[64,3,8,128]{3,2,1,0:T(8,128)S(1)}, u32[]{:S(2)}, u32[]{:S(2)}) collective-permute-start(f32[64,3,8,128]{3,2,1,0:T(8,128)S(1)} %fusion.6), channel_id=1, source_target_pairs={{0,2},{2,0},{4,6},{6,4},{8,10},{10,8},{12,14},{14,12},{1,3},{3,1},... | collective-permute-start | bytes 2359304 | tf_op jit(solution)/shard_map/ppermute | solution.py:22
  122.5 22.9 %collective-permute-start.1 = (f32[64,72]{0,1:T(8,128)S(1)}, f32[64,72]{0,1:T(8,128)S(1)}, u32[]{:S(2)}, u32[]{:S(2)}) collective-permute-start(f32[64,72]{0,1:T(8,128)S(1)} %reshape.398), channel_id=1, source_target_pairs={{0,2},{2,0},{4,6},{6,4},{8,10},{10,8},{12,14},{14,12},{1,3},{3,1},... | collective-permute-start | bytes 55304 | tf_op jit(solution)/shard_map/ppermute | solution.py:22
  146.1 1.9 copy-start.8
  156.3 17.0 %copy-start.10 = (f32[1,4096]{1,0:T(1,128)S(1)}, f32[1,4096]{1,0:T(1,128)}, u32[]{:S(2)}) copy-start(f32[1,4096]{1,0:T(1,128)} %param.30) | copy-start | bytes 49156
  159.0 89.7 %copy-start.9 = (f32[8192]{0:T(1024)S(1)}, f32[8192]{0:T(1024)}, u32[]{:S(2)}) copy-start(f32[8192]{0:T(1024)} %param.24) | copy-start | bytes 98308
  159.1 134.2 %all-gather.15.cloned.1.call-start = ((), (), s32[]{:S(2)}) async-start(), calls=%async_computation.6 | async-start | bytes 1769472 | tf_op jit(solution)/shard_map/all_gather | solution.py:191
  175.1 169.0 %all-gather.17.cloned.1.call-start = ((), (), s32[]{:S(2)}) async-start(), calls=%async_computation.7 | async-start | bytes 4456448 | tf_op jit(solution)/shard_map/all_gather | solution.py:191
  293.3 1.4 copy-start.5
  294.7 11.5 %copy-start.12 = (s32[3,64]{1,0:T(4,128)S(1)}, s32[3,64]{1,0:T(4,128)}, u32[]{:S(2)}) copy-start(s32[3,64]{1,0:T(4,128)} %param.33) | copy-start | bytes 2308
  304.1 1.2 copy-start
  306.2 50.5 %collective-permute-start.2 = (f32[192,1024]{1,0:T(8,128)}, f32[192,1024]{1,0:T(8,128)}, u32[]{:S(2)}, u32[]{:S(2)}) collective-permute-start(f32[192,1024]{1,0:T(8,128)} %dynamic-slice_bitcast_fusion), channel_id=1, source_target_pairs={{0,16},{16,0},{1,17},{17,1},{2,18},{18,2},{3,19},{19,3},{4,20},{20... | collective-permute-start | bytes 2359304 | tf_op jit(solution)/shard_map/ppermute | solution.py:256
  347.3 9.4 %copy-start.1 = (f32[2,192,1024]{2,1,0:T(8,128)S(1)}, f32[2,192,1024]{2,1,0:T(8,128)}, u32[]{:S(2)}) copy-start(f32[2,192,1024]{2,1,0:T(8,128)} %copy-done) | copy-start | bytes 4718596
Sparse Core Ops, SparseCore 0:
  10.0 47.1 all-gather.12
  59.3 44.4 all-gather.10
  107.2 64.7 reduce-scatter.4
  175.7 71.6 reduce-scatter.2
  250.0 43.2 all-gather.14
  295.3 48.7 all-gather.16

commit v2 on v1

--- a/solution.py
+++ b/solution.py
@@ -46,33 +46,30 @@
     return (values * cosine + other * sine).astype(jnp.bfloat16)
 
 
-def norm_rows(values, gain_row):
-    values = values.astype(jnp.float32)
-    scaling = lax.rsqrt(jnp.mean(values * values, axis=-1, keepdims=True) + EPSILON)
-    return (values * scaling * gain_row).astype(jnp.bfloat16)
-
-
-def project_kernel(tile, weight_count, x_ref, gain_ref, *refs):
+def row_scaling(x_ref):
+    blocks, rows, width = x_ref.shape
+
+    def add(index, total):
+        part = x_ref[index].astype(jnp.float32)
+        return total + jnp.sum(part * part, axis=-1, keepdims=True)
+
+    total = lax.fori_loop(0, blocks, add, jnp.zeros((rows, 1), jnp.float32))
+    return lax.rsqrt(total / (blocks * width) + EPSILON)
+
+
+def project_kernel(weight_count, x_ref, gain_ref, *refs):
     weights = refs[:weight_count]
     outs = refs[weight_count:-1]
     scale_ref = refs[-1]
     step = pl.program_id(0)
-    rows, depth = x_ref.shape
 
     @pl.when(step == 0)
     def _():
-        def add(index, total):
-            part = x_ref[:, pl.ds(pl.multiple_of(index * tile, tile), tile)].astype(jnp.float32)
-            return total + jnp.sum(part * part, axis=-1, keepdims=True)
-
-        total = lax.fori_loop(0, depth // tile, add, jnp.zeros((rows, 1), jnp.float32))
-        scaling = lax.rsqrt(total / depth + EPSILON)
-        scale_ref[...] = jnp.broadcast_to(scaling, scale_ref.shape)
+        scale_ref[...] = jnp.broadcast_to(row_scaling(x_ref), scale_ref.shape)
         for out in outs:
             out[...] = jnp.zeros_like(out)
 
-    columns = pl.ds(pl.multiple_of(step * tile, tile), tile)
-    normed = x_ref[:, columns].astype(jnp.float32) * scale_ref[:, :1] * gain_ref[:, columns]
+    normed = x_ref[step].astype(jnp.float32) * scale_ref[:, :1] * gain_ref[step]
     normed = normed.astype(jnp.bfloat16)
     place = 0
     for weight in weights:
@@ -87,78 +84,105 @@
                 place += 1
 
 
-def project(x, gain, weights, tile):
-    rows, depth = x.shape
-    tile = tile_of(depth, tile)
+def project(x, gain, weights):
+    blocks, rows, tile = x.shape
     specs = []
     shapes = []
     for weight in weights:
         width = weight.shape[-1]
-        if weight.ndim == 2:
+        lead = weight.shape[:-2]
+        zeros = (0,) * len(lead)
+        if weight.ndim == 4:
+            specs.append(
+                pl.BlockSpec((None, lead[1], tile, width), lambda k: (0, 0, k, 0))
+            )
+            shapes.extend([(rows, width)] * lead[1])
+        elif weight.ndim == 3:
+            specs.append(pl.BlockSpec((lead[0], tile, width), lambda k: (0, k, 0)))
+            shapes.extend([(rows, width)] * lead[0])
+        else:
             specs.append(pl.BlockSpec((tile, width), lambda k: (k, 0)))
             shapes.append((rows, width))
-        else:
-            specs.append(pl.BlockSpec((weight.shape[0], tile, width), lambda k: (0, k, 0)))
-            shapes.extend([(rows, width)] * weight.shape[0])
     return pl.pallas_call(
-        functools.partial(project_kernel, tile, len(weights)),
-        grid=(depth // tile,),
+        functools.partial(project_kernel, len(weights)),
+        grid=(blocks,),
         in_specs=[
-            pl.BlockSpec((rows, depth), lambda k: (0, 0)),
-            pl.BlockSpec((1, depth), lambda k: (0, 0)),
+            pl.BlockSpec((blocks, rows, tile), lambda k: (0, 0, 0)),
+            pl.BlockSpec((blocks, 1, tile), lambda k: (0, 0, 0)),
         ]
         + specs,
         out_specs=[pl.BlockSpec(shape, lambda k: (0, 0)) for shape in shapes],
         out_shape=[jax.ShapeDtypeStruct(shape, jnp.float32) for shape in shapes],
         scratch_shapes=[pltpu.VMEM((rows, 128), jnp.float32)],
         compiler_params=pltpu.CompilerParams(vmem_limit_bytes=VMEM_LIMIT),
-    )(x, gain, *weights)
-
-
-def out_kernel(x_ref, w_ref, o_ref):
-    o_ref[...] = jnp.dot(x_ref[...], w_ref[...], preferred_element_type=jnp.float32).astype(
-        o_ref.dtype
-    )
-
-
-def out_project(x, weight, most):
+    )(x, gain.reshape(blocks, 1, tile), *weights)
+
+
+def out_kernel(parts, x_ref, w_ref, o_ref):
+    width = w_ref.shape[1] // parts
+    for part in range(parts):
+        o_ref[part] = jnp.dot(
+            x_ref[...],
+            w_ref[:, part * width : (part + 1) * width],
+            preferred_element_type=jnp.float32,
+        ).astype(o_ref.dtype)
+
+
+def out_project(x, weight, blocks):
     rows, depth = x.shape
-    width = weight.shape[1]
-    tile = tile_of(width, most)
+    tile = weight.shape[1] // blocks
+    parts = 2 if blocks % 2 == 0 else 1
     return pl.pallas_call(
-        out_kernel,
-        grid=(width // tile,),
+        functools.partial(out_kernel, parts),
+        grid=(blocks // parts,),
         in_specs=[
             pl.BlockSpec((rows, depth), lambda n: (0, 0)),
-            pl.BlockSpec((depth, tile), lambda n: (0, n)),
+            pl.BlockSpec((depth, tile * parts), lambda n: (0, n)),
         ],
-        out_specs=pl.BlockSpec((rows, tile), lambda n: (0, n)),
-        out_shape=jax.ShapeDtypeStruct((rows, width), jnp.bfloat16),
+        out_specs=pl.BlockSpec((parts, rows, tile), lambda n: (n, 0, 0)),
+        out_shape=jax.ShapeDtypeStruct((blocks, rows, tile), jnp.bfloat16),
         compiler_params=pltpu.CompilerParams(vmem_limit_bytes=VMEM_LIMIT),
     )(x, weight)
 
 
-def logit_kernel(x_ref, w_ref, o_ref):
+def logit_kernel(x_ref, gain_ref, w_ref, o_ref, normed_ref):
+    blocks, rows, width = x_ref.shape
+
+    @pl.when((pl.program_id(0) == 0) & (pl.program_id(1) == 0))
+    def _():
+        scaling = row_scaling(x_ref)
+
+        def fill(index, carry):
+            normed = x_ref[index].astype(jnp.float32) * scaling * gain_ref[index]
+            columns = pl.ds(pl.multiple_of(index * width, width), width)
+            normed_ref[:, columns] = normed.astype(jnp.bfloat16)
+            return carry
+
+        lax.fori_loop(0, blocks, fill, 0)
+
     o_ref[...] = lax.dot_general(
-        x_ref[...], w_ref[...], (((1,), (1,)), ((), ())), preferred_element_type=jnp.float32
-    )
-
-
-def logit_project(x, table, most):
-    rows, depth = x.shape
+        normed_ref[...], w_ref[...], (((1,), (1,)), ((), ())), preferred_element_type=jnp.float32
+    )
+
+
+def logit_project(x, gain, table, most):
+    blocks, rows, block_width = x.shape
+    depth = blocks * block_width
     parts, width = table.shape[:2]
     tile = tile_of(width, most)
     return pl.pallas_call(
         logit_kernel,
         grid=(parts, width // tile),
         in_specs=[
-            pl.BlockSpec((rows, depth), lambda p, n: (0, 0)),
+            pl.BlockSpec((blocks, rows, block_width), lambda p, n: (0, 0, 0)),
+            pl.BlockSpec((blocks, 1, block_width), lambda p, n: (0, 0, 0)),
             pl.BlockSpec((None, tile, depth), lambda p, n: (p, n, 0)),
         ],
         out_specs=pl.BlockSpec((None, rows, tile), lambda p, n: (p, 0, n)),
         out_shape=jax.ShapeDtypeStruct((parts, rows, width), jnp.float32),
+        scratch_shapes=[pltpu.VMEM((rows, depth), jnp.bfloat16)],
         compiler_params=pltpu.CompilerParams(vmem_limit_bytes=VMEM_LIMIT),
-    )(x, table)
+    )(x, gain.reshape(blocks, 1, block_width), table)
 
 
 def attention_weights(cached_scores, fresh_scores, visible, causal):
@@ -177,18 +201,253 @@
     return ((cached_exp / totals).astype(jnp.bfloat16), (fresh_exp / totals).astype(jnp.bfloat16))
 
 
-def mix_rows(partial, inputs, gain, axes):
-    count = lax.axis_size(axes)
-    rows = partial.shape[0] // count
-    mixed = lax.psum_scatter(
-        partial.reshape(count, rows, partial.shape[1]), axes, scatter_dimension=0, tiled=False
-    )
-    start = lax.axis_index(axes) * rows
-    hidden = lax.dynamic_slice_in_dim(inputs, start, rows, 0).astype(jnp.float32) + mixed.astype(
-        jnp.float32
-    )
-    final = norm_rows(hidden, gain)
-    return lax.all_gather(final, axes, axis=0, tiled=False).reshape(partial.shape)
+def flips(index, bits):
+    return [bit * (1 - 2 * (lax.div(index, bit) % 2)) for bit in bits]
+
+
+def span(offsets):
+    sums = [0]
+    for offset in offsets:
+        sums = sums + [total + offset for total in sums]
+    return sums
+
+
+def link_order(size, group):
+    count = size.bit_length() - 1
+    first = list(reversed(range(count)))
+    second = [0] + list(reversed(range(1, count))) if count else []
+    return [(1 << a) + group * ((1 << b) - (1 << a)) for a, b in zip(first, second)]
+
+
+def greet(partners):
+    barrier = pltpu.get_barrier_semaphore()
+    for target in partners:
+        pl.semaphore_signal(
+            barrier, inc=1, device_id=target, device_id_type=pl.DeviceIdType.MESH
+        )
+    pl.semaphore_wait(barrier, len(partners))
+
+
+def send(source, target, sends, receives, place, device):
+    copy = pltpu.make_async_remote_copy(
+        src_ref=source,
+        dst_ref=target,
+        send_sem=sends.at[place],
+        recv_sem=receives.at[place],
+        device_id=device,
+        device_id_type=pl.DeviceIdType.MESH,
+    )
+    copy.start()
+    return copy
+
+
+def gather_kernel(size, x_ref, o_ref, local_sem, sends, receives, core_sends, core_receives):
+    group = lax.axis_index("grp")
+    mine = lax.axis_index("tp")
+    data = lax.axis_index("dp")
+    offsets = flips(mine, link_order(size, group))
+    other_core = (1 - group, mine, data)
+    greet([(group, mine + offset, data) for offset in offsets] + [other_core])
+    base = group * size
+    keep = pltpu.make_async_copy(x_ref, o_ref.at[base + mine], local_sem)
+    keep.start()
+    keep.wait()
+    held = [0]
+    place = 0
+    waiting = []
+    swaps = [
+        send(o_ref.at[base + mine], o_ref.at[base + mine], core_sends, core_receives, 0, other_core)
+    ]
+    for offset in offsets:
+        copies = []
+        for inner in held:
+            block = base + mine + inner
+            copies.append(
+                send(
+                    o_ref.at[block],
+                    o_ref.at[block],
+                    sends,
+                    receives,
+                    place,
+                    (group, mine + offset, data),
+                )
+            )
+            place += 1
+        arrived = [inner + offset for inner in held]
+        for copy, inner in zip(copies, arrived):
+            copy.wait_recv()
+            block = base + mine + inner
+            swaps.append(
+                send(
+                    o_ref.at[block],
+                    o_ref.at[block],
+                    core_sends,
+                    core_receives,
+                    len(swaps),
+                    other_core,
+                )
+            )
+        waiting.extend(copies)
+        held = held + arrived
+    for copy in waiting:
+        copy.wait_send()
+    for copy in swaps:
+        copy.wait()
+
+
+def gather_blocks(block, identity):
+    size = lax.axis_size("tp")
+    count = lax.axis_size("grp") * size
+    return pl.pallas_call(
+        functools.partial(gather_kernel, size),
+        in_specs=[pl.BlockSpec(memory_space=pltpu.VMEM)],
+        out_specs=pl.BlockSpec(memory_space=pltpu.VMEM),
+        out_shape=jax.ShapeDtypeStruct((count,) + block.shape, block.dtype),
+        scratch_shapes=[
+            pltpu.SemaphoreType.DMA(()),
+            pltpu.SemaphoreType.DMA((size,)),
+            pltpu.SemaphoreType.DMA((size,)),
+            pltpu.SemaphoreType.DMA((size,)),
+            pltpu.SemaphoreType.DMA((size,)),
+        ],
+        compiler_params=pltpu.CompilerParams(
+            collective_id=identity, has_side_effects=True, vmem_limit_bytes=VMEM_LIMIT
+        ),
+    )(block)
+
+
+def scatter_kernel(
+    size, p_ref, x_ref, o_ref, total, stage, core_box, box, core_sends, core_receives, sends, receives
+):
+    group = lax.axis_index("grp")
+    mine = lax.axis_index("tp")
+    data = lax.axis_index("dp")
+    offsets = flips(mine, list(reversed(link_order(size, group))))
+    other_core = (1 - group, mine, data)
+    greet([(group, mine + offset, data) for offset in offsets] + [other_core])
+    order = list(reversed(span(list(reversed(offsets)))))
+    swaps = [
+        send(
+            p_ref.at[(1 - group) * size + mine + inner_other],
+            core_box.at[place],
+            core_sends,
+            core_receives,
+            place,
+            other_core,
+        )
+        for place, inner_other in enumerate(
+            list(reversed(span(list(reversed(other_offsets(size, group, mine))))))
+        )
+    ]
+    copies = []
+    place = 0
+    half = size // 2
+    for index, inner in enumerate(order):
+        swaps[index].wait_recv()
+        value = p_ref[group * size + mine + inner].astype(jnp.float32)
+        value = value + core_box[index].astype(jnp.float32)
+        total[index] = value
+        if size > 1 and index < half:
+            stage[index] = value.astype(stage.dtype)
+            copies.append(
+                send(
+                    stage.at[index],
+                    box.at[place],
+                    sends,
+                    receives,
+                    place,
+                    (group, mine + offsets[0], data),
+                )
+            )
+            place += 1
+    first = half
+    start = 0
+    for phase in range(len(offsets)):
+        active = size - first
+        for index in range(active):
+            copies[start + index].wait_recv()
+            value = total[first + index] + box[start + index].astype(jnp.float32)
+            total[first + index] = value
+            if active > 1 and index < active // 2:
+                stage[first + index] = value.astype(stage.dtype)
+                copies.append(
+                    send(
+                        stage.at[first + index],
+                        box.at[place],
+                        sends,
+                        receives,
+                        place,
+                        (group, mine + offsets[phase + 1], data),
+                    )
+                )
+                place += 1
+        start += active
+        first += active // 2
+    hidden = x_ref[...].astype(jnp.float32) + total[size - 1]
+    o_ref[...] = hidden.astype(o_ref.dtype)
+    for copy in copies + swaps:
+        copy.wait_send()
+
+
+def other_offsets(size, group, mine):
+    return flips(mine, list(reversed(link_order(size, 1 - group))))
+
+
+def scatter_blocks(partial, inputs, identity):
+    size = lax.axis_size("tp")
+    block = inputs.shape
+    whole = pl.BlockSpec(memory_space=pltpu.VMEM)
+    return pl.pallas_call(
+        functools.partial(scatter_kernel, size),
+        in_specs=[whole, whole],
+        out_specs=whole,
+        out_shape=jax.ShapeDtypeStruct(block, inputs.dtype),
+        scratch_shapes=[
+            pltpu.VMEM((size,) + block, jnp.float32),
+            pltpu.VMEM((size,) + block, partial.dtype),
+            pltpu.VMEM((size,) + block, partial.dtype),
+            pltpu.VMEM((size,) + block, partial.dtype),
+            pltpu.SemaphoreType.DMA((size,)),
+            pltpu.SemaphoreType.DMA((size,)),
+            pltpu.SemaphoreType.DMA((size,)),
+            pltpu.SemaphoreType.DMA((size,)),
+        ],
+        compiler_params=pltpu.CompilerParams(
+            collective_id=identity, has_side_effects=True, vmem_limit_bytes=VMEM_LIMIT
+        ),
+    )(partial, inputs)
+
+
+def share_kernel(size, count, x_ref, o_ref, sends, receives):
+    data = lax.axis_index("dp")
+    mine = lax.axis_index("grp") * size + lax.axis_index("tp")
+    others = [(mine + step) % count for step in range(1, count)]
+    devices = [(other // size, other % size, data) for other in others]
+    greet(devices)
+    copies = [
+        send(x_ref, o_ref.at[mine], sends, receives, place, device)
+        for place, device in enumerate(devices)
+    ]
+    o_ref[mine] = x_ref[...]
+    for copy in copies:
+        copy.wait()
+
+
+def share_small(values, identity):
+    size = lax.axis_size("tp")
+    count = lax.axis_size("grp") * size
+    whole = pl.BlockSpec(memory_space=pltpu.VMEM)
+    return pl.pallas_call(
+        functools.partial(share_kernel, size, count),
+        in_specs=[whole],
+        out_specs=whole,
+        out_shape=jax.ShapeDtypeStruct((count,) + values.shape, values.dtype),
+        scratch_shapes=[
+            pltpu.SemaphoreType.DMA((count - 1,)),
+            pltpu.SemaphoreType.DMA((count - 1,)),
+        ],
+        compiler_params=pltpu.CompilerParams(collective_id=identity, has_side_effects=True),
+    )(values)
 
 
 def body(
@@ -217,20 +476,20 @@
     group_size = base_query.shape[1] // slice_width
     slice_index = lax.axis_index("tp") % share_count
     first_pair = slice_index * (slice_width // 2)
-    block_index = lax.axis_index(("grp", "tp"))
+    block_index = lax.axis_index("grp") * lax.axis_size("tp") + lax.axis_index("tp")
     vocab_width = base_unembed.shape[0]
     small_heads = small_projections.shape[3] // HD
-    every = ("grp", "tp")
-    small_full = lax.all_gather(small_inputs[0], "tp", axis=2, tiled=True)
-    small_full = small_full.reshape(total_rows, -1)
-    base_full = lax.all_gather(base_inputs, every, axis=2, tiled=True).reshape(total_rows, -1)
+    small_block = small_inputs.reshape(total_rows, -1)
+    base_block = base_inputs.reshape(total_rows, -1)
+    small_full = lax.all_gather(small_block, "tp", axis=0)
+    base_full = gather_blocks(base_block, 0)
     positions = (jnp.arange(STEPS)[:, None] + lengths[None, :]).reshape(-1)
     visible = (jnp.arange(CACHE)[None, :] < lengths[:, None])[:, None, None, :]
     step_range = jnp.arange(STEPS)
     causal = step_range[None, :] <= step_range[:, None]
 
     small_q, small_k, small_v = project(
-        small_full, small_norm_gain, [small_projections[0]], 512
+        small_full, small_norm_gain, [small_projections]
     )
     cosine, sine = rotation_tables(positions, 0, HD, HD)
     by_head = (STEPS, row_count, small_heads, HD)
@@ -247,16 +506,18 @@
         "rhsn,nrhd->srhd", fresh, small_v, preferred_element_type=jnp.float32
     )
     heads = heads.astype(jnp.bfloat16).reshape(total_rows, small_heads * HD)
-    small_partial = out_project(heads, small_output[0], 1024)
-    small_final = mix_rows(small_partial, small_full, small_final_gain[0], "tp")
-    small_logits = logit_project(small_final, small_unembed[0], 512)
+    small_partial = out_project(heads, small_output[0], small_full.shape[0])
+    small_mixed = lax.psum_scatter(small_partial, "tp", scatter_dimension=0, tiled=False)
+    small_hidden = small_block.astype(jnp.float32) + small_mixed.astype(jnp.float32)
+    small_hidden = lax.all_gather(small_hidden.astype(jnp.bfloat16), "tp", axis=0)
+    small_logits = logit_project(small_hidden, small_final_gain, small_unembed[0], 512)
     group = lax.axis_index("grp")
     own = lax.dynamic_index_in_dim(small_logits, group, 0, keepdims=False)
     theirs = lax.dynamic_index_in_dim(small_logits, 1 - group, 0, keepdims=False)
     received = lax.ppermute(theirs, "grp", [(0, 1), (1, 0)])
 
     query, new_key, new_value = project(
-        base_full, base_norm_gain[None], [base_query, base_keys_values], 1024
+        base_full, base_norm_gain, [base_query, base_keys_values]
     )
     cosine, sine = rotation_tables(positions, first_pair, slice_width, HD)
     query = rotate(query, cosine, sine).reshape(STEPS, row_count, group_size, slice_width)
@@ -274,9 +535,9 @@
         "rsgn,nrd->srgd", fresh, new_value, preferred_element_type=jnp.float32
     )
     heads = heads.astype(jnp.bfloat16).reshape(total_rows, group_size * slice_width)
-    partial = out_project(heads, base_output, 1024)
-    final_rows = mix_rows(partial, base_full, base_final_gain, every)
-    base_logits = logit_project(final_rows, base_unembed[None], 256)[0]
+    partial = out_project(heads, base_output, base_full.shape[0])
+    hidden = gather_blocks(scatter_blocks(partial, base_block, 1), 2)
+    base_logits = logit_project(hidden, base_final_gain, base_unembed[None], 256)[0]
     gap = jnp.where(group == 0, own - received, received - own)
     steered = base_logits + gap
 
@@ -285,7 +546,9 @@
     token_local = next_tokens.reshape(-1) - block_index * vocab_width
     token_hit = jnp.arange(vocab_width)[None, :] == token_local[:, None]
     picked = jnp.sum(jnp.where(token_hit, steered, 0.0), axis=-1)
-    stats = lax.all_gather(jnp.stack([local_max, local_total, picked]), every, axis=0)
+    packed = jnp.stack([local_max, local_total, picked])
+    packed = jnp.pad(packed, ((0, -3 % 8), (0, -total_rows % 128)))
+    stats = share_small(packed, 3)[:, :3, :total_rows]
     row_max = jnp.max(stats[:, 0], axis=0)
     exp_total = jnp.sum(stats[:, 1] * jnp.exp(stats[:, 0] - row_max[None]), axis=0)
     log_norm = row_max + jnp.log(exp_total)

time: 398 us -> 324 us (0.81)
  waiting for transfers between devices: 234 us -> 72.6 us
  Pallas kernels: 49 us -> 171 us
  blocking collectives: 30.4 us -> 0 us
  local copies, waits for them, and re-layouts: 33.3 us -> 28.8 us
    pallas_call x4 -> x8, Pallas kernels: 30.2 us -> 148 us  [the longest x2 74.3 us: gather_blocks(): pl.pallas_call(functools.partial(gather_kernel, size), in_specs=[pl.Block...]
    reduce_scatter x2 -> x1, waiting for transfers between devices: 85.2 us -> 4.91 us  [body(): lax.psum_scatter(small_partial, 'tp', scatter_dimension=0, tiled=False)]
    all_gather x4 -> x2, waiting for transfers between devices: 125 us -> 51.9 us  [the longest x1 35.5 us: body(): small_full = lax.all_gather(small_block, 'tp', axis=0)]
    all_gather x1 -> x0, blocking collectives: 30.4 us -> none  [body(): lax.all_gather(jnp.stack([local_max, local_total, picked]), every, axis=0)]
    ppermute x2, waiting for transfers between devices: 22.1 us -> 15.2 us  [partner(): lax.ppermute(array, axis, [(i, i ^ 1 << bit) for i in range(lax.axis_size...]
    unnamed x29 -> x40, local copies, waits for them, and re-layouts: 14 us -> 9.72 us
  transfers between devices with their start and end apart: 9 -> 6, of which waited for: 7 -> 4; matrix products, arithmetic and copies ran while one was open for 14% -> 10% of each run, Pallas kernels for 12% -> 42%
where the time goes in v2:
time: 324 us; the launch traced here: 323 us
  Pallas kernels  171 us (53%)
  waiting for transfers between devices  72.6 us (22%)
  local copies, waits for them, and re-layouts  28.8 us (9%)
  matrix products  18.8 us (6%)
  other arithmetic  15.3 us (5%)
  between operations  14.3 us (4%)
    pallas_call x2, Pallas kernels, gather_blocks(): pl.pallas_call(functools.partial(gather_kernel, size), in_specs=[pl.Block...  74.3 us
    all_gather x1, waiting for transfers between devices, body(): small_full = lax.all_gather(small_block, 'tp', axis=0)  35.5 us
    pallas_call x1, Pallas kernels, scatter_blocks(): pl.pallas_call(functools.partial(scatter_kernel, size), in_specs=[whole,...  26 us
    pallas_call x2, Pallas kernels, project(): pl.pallas_call(functools.partial(project_kernel, len(weights)), grid=(blo...  24.7 us
    pallas_call x2, Pallas kernels, logit_project(): pl.pallas_call(logit_kernel, grid=(parts, width // tile), in_specs=[pl.Bl...  22.6 us
    all_gather x1, waiting for transfers between devices, body(): lax.all_gather(small_hidden.astype(jnp.bfloat16), 'tp', axis=0)  16.4 us
    ppermute x2, waiting for transfers between devices, partner(): lax.ppermute(array, axis, [(i, i ^ 1 << bit) for i in range(lax.axis_size...  15.2 us
    pallas_call x1, Pallas kernels, share_small(): pl.pallas_call(functools.partial(share_kernel, size, count), in_specs=[wh...  12.9 us
  transfers between devices with their start and end apart: 6, of which 4 were waited for; matrix products, arithmetic and copies ran while one was open for 10% of the time, Pallas kernels for 42%

profile of v2, /device:TPU:0, one launch (start us, length us, event | category | flops | bytes accessed | tf_op | source)
XLA Modules:
  0.0 322.9 jit_solution(7284579677675783676)
XLA Ops:
  9.9 11.7 %fusion.66 = (bf16[1,1,64,512,128]{4,3,2,1,0:T(8,128)(2,1)}, bf16[1,1,64,512,128]{4,3,2,1,0:T(8,128)(2,1)}) fusion(bf16[1,2,64,512,128]{4,3,2,1,0:T(8,128)(2,1)} %param.29), kind=kLoop, calls=%fused_computation.128 | loop fusion | bytes 33554432 | tf_op jit(solution)/shard_map/slice | solution.py:500
  21.6 35.5 %all-gather.3.cloned.1.call-done.x_ref = bf16[8,192,512]{2,1,0:T(8,128)(2,1)} async-done(((bf16[1,192,512]{2,1,0:T(8,128)(2,1)}), bf16[8,192,512]{2,1,0:T(8,128)(2,1)}) %all-gather.3.cloned.1.call-update) | async-done | bytes 1572880 | tf_op jit(solution)/shard_map/all_gather | solution.py:484
  57.1 1.4 copy-done.3
  58.5 9.7 %shard_map.182 = (f32[192,512]{1,0:T(8,128)S(1)}, f32[192,512]{1,0:T(8,128)S(1)}, f32[192,512]{1,0:T(8,128)S(1)}) custom-call(bf16[8,192,512]{2,1,0:T(8,128)(2,1)S(1)} %copy-done.3, f32[8,1,512]{2,1,0:T(1,128)S(1)} %bitcast.119, bf16[1,3,4096,512]{3,2,1,0:T(8,128)(2,1)} %refs_0_.3), custom_call_target="tpu_custom_call" | custom-call | tf_op jit(solution)/shard_map/pallas_call | solution.py:106
  70.2 5.8 %fusion.75 = (f32[64,4,3]{2,1,0:T(4,128)S(1)}, f32[64,4,3,128]{3,2,1,0:T(4,128)S(1)}) fusion(bf16[64,4,128,128]{3,2,1,0:T(8,128)(2,1)} %bitcast.121, bf16[3,64,4,128]{3,2,1,0:T(4,128)(2,1)S(1)} %reshape.395, pred[64,128]{1,0:T(8,128)(4,1)S(1)} %iota_compare_fusion.1), kind=kOutput, calls=%fused_computation.137 | convolution fusion | flops 25459968 | bytes 8989696 | tf_op jit(solution)/shard_map/srhd,rhdl->rhsl/dot_general | solution.py:501
  78.2 8.1 %fusion.4 = bf16[3,64,4,128]{3,0,2,1:T(4,128)(2,1)S(1)} fusion(f32[3,64,4,128]{3,0,2,1:T(4,128)S(1)} %convolution_bitcast_fusion.2, bf16[64,4,128,128]{3,2,1,0:T(8,128)(2,1)} %bitcast.124, f32[64,4,3,128]{3,2,1,0:T(4,128)S(1)} %get-tuple-element.54, f32[64,4,3]{2,1,0:T(4,128)S(1)} %add.176, f32[64,4,3]{2,1,0:T(4,128)S(1)} %max.17), kind=kOutput, calls=%fused_computation.9 | convolution fusion | flops 25657344 | bytes 9377792 | tf_op jit(solution)/shard_map/rhsl,rhdl->srhd/dot_general | solution.py:504
  86.4 2.9 shard_map.183
  89.6 44.3 %shard_map.176.x_ref = bf16[16,192,512]{2,1,0:T(8,128)(2,1)S(1)} custom-call(bf16[192,512]{1,0:T(8,128)(2,1)S(1)} %bitcast.115), custom_call_target="tpu_custom_call" | custom-call | tf_op jit(solution)/shard_map/pallas_call | solution.py:301
  133.9 4.8 %copy.137.refs_1_ = bf16[2,8192,64]{2,1,0:T(8,128)(2,1)} copy(bf16[2,8192,64]{1,2,0:T(8,128)(2,1)} %param.21) | data formatting | bytes 4194304 | tf_op args[4]
  139.5 15.0 %shard_map.177 = (f32[192,512]{1,0:T(8,128)S(1)}, f32[192,64]{1,0:T(8,128)S(1)}, f32[192,64]{1,0:T(8,128)S(1)}) custom-call(bf16[16,192,512]{2,1,0:T(8,128)(2,1)S(1)} %shard_map.176.x_ref, f32[16,1,512]{2,1,0:T(1,128)S(1)} %bitcast.117, bf16[8192,512]{1,0:T(8,128)(2,1)} %refs_0_.2, bf16[2,8192,64]{2,1,0:T(8,128)(2,1)} %copy.137.refs_1_), custom_call_target="tpu_custom_call" | custom-call | tf_op jit(solution)/shard_map/pallas_call | solution.py:106
  155.8 4.9 %reduce-scatter.2.cloned.1.call-done = bf16[1,192,512]{2,1,0:T(8,128)(2,1)} async-done(((bf16[8,192,512]{2,1,0:T(8,128)(2,1)}), bf16[1,192,512]{2,1,0:T(8,128)(2,1)}) %reduce-scatter.2.cloned.1.call-update) | async-done | bytes 196624 | tf_op jit(solution)/shard_map/reduce_scatter | solution.py:510
  160.8 1.7 add_convert_fusion
  162.5 1.1 fusion.74
  163.6 1.1 fusion.67
  164.7 1.3 fusion.40
  167.3 1.6 fusion.6
  169.6 1.3 fusion.23
  171.2 1.5 collective-permute-start.1
  173.9 15.2 %collective-permute-done.1 = f32[64,72]{0,1:T(8,128)S(1)} collective-permute-done((f32[64,72]{0,1:T(8,128)S(1)}, f32[64,72]{0,1:T(8,128)S(1)}, u32[]{:S(2)}, u32[]{:S(2)}) %collective-permute-start.1) | collective-permute-done | bytes 18464 | tf_op jit(solution)/shard_map/ppermute | solution.py:22
  189.8 1.5 fusion.65
  191.9 16.4 %all-gather.5.cloned.1.call-done.x_ref = bf16[8,192,512]{2,1,0:T(8,128)(2,1)} async-done(((bf16[1,192,512]{2,1,0:T(8,128)(2,1)}), bf16[8,192,512]{2,1,0:T(8,128)(2,1)}) %all-gather.5.cloned.1.call-update) | async-done | bytes 1572880 | tf_op jit(solution)/shard_map/all_gather | solution.py:512
  208.2 1.4 copy-done.2
  209.7 10.7 %shard_map.184 = f32[2,192,1024]{2,1,0:T(8,128)S(1)} custom-call(bf16[8,192,512]{2,1,0:T(8,128)(2,1)S(1)} %copy-done.2, f32[8,1,512]{2,1,0:T(1,128)S(1)} %bitcast.120, bf16[2,1024,4096]{2,1,0:T(8,128)(2,1)} %bitcast.123), custom_call_target="tpu_custom_call" | custom-call | tf_op jit(solution)/shard_map/pallas_call | solution.py:173
  220.4 0.9 dynamic-slice_bitcast_fusion
  223.3 7.1 %shard_map.178.p_ref = bf16[16,192,512]{2,1,0:T(8,128)(2,1)S(1)} custom-call(bf16[192,512]{1,0:T(8,128)(2,1)S(1)} %reshape.391.x_ref, bf16[512,8192]{1,0:T(8,128)(2,1)} %w_ref.1), custom_call_target="tpu_custom_call" | custom-call | tf_op jit(solution)/shard_map/pallas_call | solution.py:135
  230.4 26.0 %shard_map.179.x_ref = bf16[192,512]{1,0:T(8,128)(2,1)S(1)} custom-call(bf16[16,192,512]{2,1,0:T(8,128)(2,1)S(1)} %shard_map.178.p_ref, bf16[192,512]{1,0:T(8,128)(2,1)S(1)} %bitcast.116), custom_call_target="tpu_custom_call" | custom-call | tf_op jit(solution)/shard_map/pallas_call | solution.py:400
  256.5 29.9 %shard_map.180.x_ref = bf16[16,192,512]{2,1,0:T(8,128)(2,1)S(1)} custom-call(bf16[192,512]{1,0:T(8,128)(2,1)S(1)} %shard_map.179.x_ref), custom_call_target="tpu_custom_call" | custom-call | tf_op jit(solution)/shard_map/pallas_call | solution.py:301
  286.4 11.9 %shard_map.181 = f32[1,192,1024]{2,1,0:T(8,128)S(1)} custom-call(bf16[16,192,512]{2,1,0:T(8,128)(2,1)S(1)} %shard_map.180.x_ref, f32[16,1,512]{2,1,0:T(1,128)S(1)} %bitcast.118, bf16[1,1024,8192]{2,1,0:T(8,128)(2,1)} %bitcast.122), custom_call_target="tpu_custom_call" | custom-call | tf_op jit(solution)/shard_map/pallas_call | solution.py:173
  298.3 1.4 fusion.62
  300.6 12.9 %shard_map.185 = f32[16,8,256]{2,1,0:T(8,128)} custom-call(f32[8,256]{1,0:T(8,128)} %select_maximum_fusion.x_ref), custom_call_target="tpu_custom_call" | custom-call | tf_op jit(solution)/shard_map/pallas_call | solution.py:440
  313.6 1.1 slice_reduce_fusion
  314.7 1.0 broadcast_subtract_fusion
  (111 shorter events, 17.4 us)
Async XLA Ops:
  7.2 49.9 %all-gather.3.cloned.1.call-start = ((), (), s32[]{:S(2)}) async-start(), calls=%async_computation.1 | async-start | bytes 1769472 | tf_op jit(solution)/shard_map/all_gather | solution.py:484
  7.9 152.9 %reduce-scatter.2.cloned.1.call-start = ((), (), s32[]{:S(2)}) async-start(), calls=%async_computation.2 | async-start | bytes 1769472 | tf_op jit(solution)/shard_map/reduce_scatter | solution.py:510
  8.7 68.5 %copy-start.15 = (pred[3,3]{1,0:T(4,128)(4,1)}, pred[3,3]{1,0:T(4,128)(4,1)S(1)}, u32[]{:S(2)}) copy-start(pred[3,3]{1,0:T(4,128)(4,1)S(1)} %iota_compare_fusion.4) | copy-start | bytes 31
  9.5 60.7 %copy-start.13 = (pred[64,128]{1,0:T(8,128)(4,1)}, pred[64,128]{1,0:T(8,128)(4,1)S(1)}, u32[]{:S(2)}) copy-start(pred[64,128]{1,0:T(8,128)(4,1)S(1)} %iota_compare_fusion.1) | copy-start | bytes 24580
  9.9 47.2 %copy-start.10 = (f32[1,4096]{1,0:T(1,128)S(1)}, f32[1,4096]{1,0:T(1,128)}, u32[]{:S(2)}) copy-start(f32[1,4096]{1,0:T(1,128)} %param.26) | copy-start | bytes 49156
  57.1 1.4 copy-start.3
  77.7 8.7 %copy-start = (bf16[1,512,4096]{2,1,0:T(8,128)(2,1)S(1)}, bf16[1,512,4096]{2,1,0:T(8,128)(2,1)}, u32[]{:S(2)}) copy-start(bf16[1,512,4096]{2,1,0:T(8,128)(2,1)} %param.28) | copy-start | bytes 12582916
  78.1 11.4 %copy-start.4 = (bf16[3,64,512]{2,1,0:T(8,128)(2,1)S(1)}, bf16[3,64,512]{2,1,0:T(8,128)(2,1)}, u32[]{:S(2)}) copy-start(bf16[3,64,512]{2,1,0:T(8,128)(2,1)} %param.17) | copy-start | bytes 589828
  89.3 118.9 %all-gather.5.cloned.1.call-start = ((), (), s32[]{:S(2)}) async-start(), calls=%async_computation.3 | async-start | bytes 1769472 | tf_op jit(solution)/shard_map/all_gather | solution.py:512
  138.7 0.8 copy-start.8
  154.5 0.6 copy-start.1
  155.2 0.6 copy-start.6
  155.8 16.8 %copy-start.18 = (s32[3,64]{1,0:T(4,128)S(1)}, s32[3,64]{1,0:T(4,128)}, u32[]{:S(2)}) copy-start(s32[3,64]{1,0:T(4,128)} %param.33) | copy-start | bytes 2308
  155.8 33.5 %copy-start.16 = (pred[3,3]{1,0:T(4,128)(4,1)S(1)}, pred[3,3]{1,0:T(4,128)(4,1)}, u32[]{:S(2)}) copy-start(pred[3,3]{1,0:T(4,128)(4,1)} %copy-done.15) | copy-start | bytes 31
  155.8 16.8 %copy-start.7 = (f32[192,64]{1,0:T(8,128)S(1)}, f32[192,64]{1,0:T(8,128)}, u32[]{:S(2)}) copy-start(f32[192,64]{1,0:T(8,128)} %copy-done.6) | copy-start | bytes 147460
  166.2 42.1 %copy-start.11 = (f32[1,4096]{1,0:T(1,128)S(1)}, f32[1,4096]{1,0:T(1,128)}, u32[]{:S(2)}) copy-start(f32[1,4096]{1,0:T(1,128)} %param.30) | copy-start | bytes 49156
  168.9 20.8 %collective-permute-start = (f32[64,3,8,128]{3,2,1,0:T(8,128)S(1)}, f32[64,3,8,128]{3,2,1,0:T(8,128)}, u32[]{:S(2)}, u32[]{:S(2)}) collective-permute-start(f32[64,3,8,128]{3,2,1,0:T(8,128)S(1)} %fusion.6), channel_id=1, source_target_pairs={{0,2},{2,0},{4,6},{6,4},{8,10},{10,8},{12,14},{14,12},{1,3},{3,1},... | collective-permute-start | bytes 2359304 | tf_op jit(solution)/shard_map/ppermute | solution.py:22
  171.2 17.9 %collective-permute-start.1 = (f32[64,72]{0,1:T(8,128)S(1)}, f32[64,72]{0,1:T(8,128)S(1)}, u32[]{:S(2)}, u32[]{:S(2)}) collective-permute-start(f32[64,72]{0,1:T(8,128)S(1)} %reshape.388), channel_id=1, source_target_pairs={{0,2},{2,0},{4,6},{6,4},{8,10},{10,8},{12,14},{14,12},{1,3},{3,1},... | collective-permute-start | bytes 55304 | tf_op jit(solution)/shard_map/ppermute | solution.py:22
  208.2 1.4 copy-start.2
  209.7 12.1 %copy-start.14 = (bf16[192,64]{1,0:T(8,128)(2,1)S(1)}, bf16[192,64]{1,0:T(8,128)(2,1)}, u32[]{:S(2)}) copy-start(bf16[192,64]{1,0:T(8,128)(2,1)} %convert_element_type.87) | copy-start | bytes 73732
  209.7 12.5 %copy-start.12 = (bf16[2,64,64,128]{3,2,1,0:T(8,128)(2,1)S(1)}, bf16[2,64,64,128]{3,2,1,0:T(8,128)(2,1)}, u32[]{:S(2)}) copy-start(bf16[2,64,64,128]{3,2,1,0:T(8,128)(2,1)} %param.23) | copy-start | bytes 6291460
  221.3 77.0 %collective-permute-start.2 = (f32[192,1024]{1,0:T(8,128)}, f32[192,1024]{1,0:T(8,128)}, u32[]{:S(2)}, u32[]{:S(2)}) collective-permute-start(f32[192,1024]{1,0:T(8,128)} %dynamic-slice_bitcast_fusion), channel_id=1, source_target_pairs={{0,16},{16,0},{1,17},{17,1},{2,18},{18,2},{3,19},{19,3},{4,20},{20... | collective-permute-start | bytes 2359304 | tf_op jit(solution)/shard_map/ppermute | solution.py:517
  222.9 7.5 %copy-start.5 = (bf16[3,64,512]{2,1,0:T(8,128)(2,1)S(1)}, bf16[3,64,512]{2,1,0:T(8,128)(2,1)}, u32[]{:S(2)}) copy-start(bf16[3,64,512]{2,1,0:T(8,128)(2,1)} %param.17) | copy-start | bytes 589828
  223.3 63.1 %copy-start.9 = (f32[8192]{0:T(1024)S(1)}, f32[8192]{0:T(1024)}, u32[]{:S(2)}) copy-start(f32[8192]{0:T(1024)} %param.24) | copy-start | bytes 98308
  286.4 13.2 %copy-start.17 = (s32[192]{0:T(256)S(1)}, s32[192]{0:T(256)}, u32[]{:S(2)}) copy-start(s32[192]{0:T(256)} %sub.114) | copy-start | bytes 2308
Sparse Core Ops, SparseCore 0:
  10.2 46.8 all-gather.2
  89.5 71.2 reduce-scatter.1
  163.5 44.6 all-gather.4
